TPU v7x, 32 devices: a whole 2x2x4 slice. The times are simulated.
32 devices in a mesh: dp: 16 (over z, y, x), sub: 2 (over core).
Axes of the slice: x: 2, y: 2, z: 4, core: 2. Of those that a mesh axis runs over, the one named last changes fastest.
Arguments:
- points: bfloat16 [16384, 256], P(('dp', 'sub'))
- candidates: int32 [4, 768], replicated, may hold values from 0 to 16383, as said below
- owner_slot: int32 [3072], replicated, may hold values from 0 to 3071, each once
Outputs:
- centroids: float32 [3072, 256], P(('dp', 'sub'))
- masses: float32 [3072], P(('dp', 'sub'))
- min_dist: float32 [16384], P(('dp', 'sub'))
Inputs may be any that keep to these rules, and one draw needn't show every extreme that they name: In each round the candidates are distinct rows; no device's block of 512 rows holds more than 96 candidates of one round, and in each round some device's block holds exactly 96.
All inputs are finite; a program needn't handle non-finite values.
Results may differ from a plain program's by a relative error of at most 0.00055.
Values may be sent and summed in bfloat16 or wider, within the bound.
No kernel may reach another device: no remote copies, remote signals or barrier semaphores. Data moves between devices by JAX's collectives and lax.ppermute only.
A program may use at most 64 MiB of HBM per device.

v0:
```python
import jax
import jax.numpy as jnp
from jax import lax
from jax.sharding import PartitionSpec as P


def pick_rows(round_rows, points, my_device):
    row_count = points.shape[0]
    flat_rows = round_rows.reshape(-1)
    owner_dev = flat_rows // row_count
    local_row = flat_rows % row_count
    mine = owner_dev == my_device
    picked = jnp.where(
        mine[:, None], points[local_row].astype(jnp.float32), jnp.zeros((), jnp.float32)
    )
    return lax.psum(picked, ("dp", "sub")).astype(jnp.bfloat16)


def on_device(points, candidates, owner_slot):
    row_count = points.shape[0]
    width_dim = points.shape[1]
    round_count = candidates.shape[0]
    cand_count = candidates.shape[1]
    my_device = lax.axis_index(("dp", "sub"))
    block_rows = min(512, row_count)
    point_norm = jnp.sum(points.astype(jnp.float32) ** 2, axis=1)
    all_chosen = pick_rows(candidates, points, my_device)
    chosen_list = [
        all_chosen[which_round * cand_count : (which_round + 1) * cand_count]
        for which_round in range(round_count)
    ]
    nearest_parts = [jnp.full((block_rows,), 3e38, jnp.float32)]
    sums_parts = []
    mass_parts = []
    for which_round in range(round_count):
        chosen = chosen_list[which_round]
        cand_norm = jnp.sum(chosen.astype(jnp.float32) ** 2, axis=1)
        dots = lax.dot_general(
            points, chosen, (((1,), (1,)), ((), ())), preferred_element_type=jnp.float32
        )
        dist = point_norm[:, None] + cand_norm[None, :] - 2.0 * dots
        nearest_parts[0] = jnp.minimum(nearest_parts[0], jnp.min(dist, axis=1))
        kernel = jnp.exp(-dist / 0.25).astype(jnp.bfloat16)
        sums_round = lax.dot_general(
            kernel, points, (((0,), (0,)), ((), ())), preferred_element_type=jnp.float32
        )
        mass_round = jnp.sum(kernel.astype(jnp.float32), axis=0)
        sums_parts.append(sums_round)
        mass_parts.append(mass_round)
    partial_sums = jnp.concatenate(sums_parts, axis=0)
    partial_mass = jnp.concatenate(mass_parts, axis=0)
    total_rows = partial_sums.shape[0]
    placed_sums = jnp.zeros((total_rows, width_dim), jnp.float32).at[owner_slot].set(partial_sums)
    placed_mass = jnp.zeros((total_rows,), jnp.float32).at[owner_slot].set(partial_mass)
    summed, masses = (
        lax.psum_scatter(placed_sums, ("dp", "sub"), scatter_dimension=0, tiled=True),
        lax.psum_scatter(placed_mass, ("dp", "sub"), scatter_dimension=0, tiled=True),
    )
    centroids = summed / masses[:, None]
    min_dist = nearest_parts[0]
    return (centroids, masses, min_dist)


def solution(mesh):
    placed = (P(("dp", "sub"), None), P(), P())
    return jax.shard_map(
        on_device,
        mesh=mesh,
        in_specs=placed,
        out_specs=(P(("dp", "sub"), None), P(("dp", "sub")), P(("dp", "sub"))),
        check_vma=False,
    )
```

profile of v0, /device:TPU:0, one launch (start us, length us, event | category | flops | bytes accessed | tf_op | source)
XLA Modules:
  0.0 239.9 jit_solution(6603793152134570887)
XLA Ops:
  7.2 0.0 copy-start
  7.2 0.0 reduce-scatter.2.cloned.1.call-start
  7.2 0.7 compare_select_fusion.3
  8.0 0.7 reshape.107
  8.7 0.7 copy.6
  9.4 0.1 compare_select_fusion
  9.5 1.1 multiply_reduce_fusion.4
  10.6 0.0 copy-done
  10.6 13.0 %gather_fusion = bf16[3072,256]{1,0:T(8,128)(2,1)} fusion(bf16[512,256]{1,0:T(8,128)(2,1)S(1)} %copy-done, s32[3072]{0:T(1024)S(1)} %broadcast_clamp_fusion), kind=kCustom, calls=%fused_computation | custom fusion | bytes 3158016 | tf_op jit(solution)/shard_map/gather | solution.py:14
  23.6 2.7 %convert_select_fusion = f32[3072,256]{1,0:T(8,128)S(1)} fusion(bf16[3072,256]{1,0:T(8,128)(2,1)} %gather_fusion, pred[3072]{0:T(1024)(128)(4,1)S(1)} %fusion.18), kind=kLoop, calls=%fused_computation.11 | loop fusion | flops 1572864 | bytes 4721664 | tf_op jit(solution)/shard_map/jit(_where)/select_n | solution.py:13
  26.3 80.7 %all-reduce.2 = bf16[3072,256]{1,0:T(8,128)(2,1)} all-reduce(f32[3072,256]{1,0:T(8,128)S(1)} %convert_select_fusion), channel_id=1, replica_groups=mesh['dp'=16,'sub'=2] {'dp','sub'}, use_global_device_ids=true, to_apply=%region_1.2 | all-reduce | flops 786432 | bytes 4718592 | tf_op jit(solution)/shard_map/psum | solution.py:16
  107.0 0.0 copy-start.1
  107.0 1.9 multiply_reduce_fusion.3
  108.9 0.0 copy-done.1
  109.0 0.7 fusion.30
  109.6 0.4 fusion.16
  110.0 0.7 fusion.29
  110.7 0.4 fusion.15
  111.1 0.7 fusion.28
  111.8 0.4 fusion.14
  112.2 0.7 fusion.27
  112.9 0.4 fusion.13
  113.3 17.1 %scatter_custom_fusion = f32[3072,256]{1,0:T(8,128)} fusion(s32[3072]{0:T(1024)S(1)} %compare_select_fusion.3, f32[768,256]{1,0:T(8,128)S(1)} %fusion.16, f32[]{:T(128)} %constant.61, f32[768,256]{1,0:T(8,128)S(1)} %fusion.15, f32[768,256]{1,0:T(8,128)S(1)} %fusion.14, f32[768,256]{1,0:T(8,128)S(1)} %fusion.13, f32[]{:T(128)} %constant.43.clone.1), kind=kCustom, calls=%fused_computation.3 | custom fusion | flops 2359296 | bytes 6291464 | tf_op jit(solution)/shard_map/scatter | solution.py:53
  130.4 0.0 reduce-scatter.2.cloned.1.call-update
  130.4 11.8 %scatter_custom_fusion.1 = f32[3072]{0:T(1024)S(1)} fusion(s32[3072]{0:T(1024)S(1)} %compare_select_fusion.3, f32[3072]{0:T(1024)S(1)} %pad_maximum_fusion, f32[]{:T(128)} %constant.43.clone.1), kind=kCustom, calls=%fused_computation.55 | custom fusion | bytes 12292 | tf_op jit(solution)/shard_map/scatter | solution.py:54
  142.3 38.4 %all-reduce = f32[3072]{0:T(1024)S(1)} all-reduce(f32[3072]{0:T(1024)S(1)} %scatter_custom_fusion.1), channel_id=3, replica_groups=mesh['dp'=16,'sub'=2] {'dp','sub'}, use_global_device_ids=true, to_apply=%region_13.14.clone | all-reduce | flops 3072 | bytes 24576
  180.6 0.1 dynamic-slice
  180.7 0.0 copy-start.2
  180.7 0.6 minimum_minimum_fusion
  181.3 50.1 %reduce-scatter.2.cloned.1.call-done = f32[96,256]{1,0:T(8,128)} async-done(((f32[3072,256]{1,0:T(8,128)}), f32[96,256]{1,0:T(8,128)}) %reduce-scatter.2.cloned.1.call-update) | async-done | bytes 98320 | tf_op jit(solution)/shard_map/reduce_scatter | solution.py:56
  231.4 1.6 broadcast_divide_fusion
  233.0 0.0 copy-done.2
  (3 shorter events, 0.0 us)
Async XLA Ops:
  7.2 3.4 %copy-start = (bf16[512,256]{1,0:T(8,128)(2,1)S(1)}, bf16[512,256]{1,0:T(8,128)(2,1)}, u32[]{:S(2)}) copy-start(bf16[512,256]{1,0:T(8,128)(2,1)} %param.3) | copy-start | bytes 786436
  7.2 224.2 %reduce-scatter.2.cloned.1.call-start = ((), (), s32[]{:S(2)}) async-start(), calls=%async_computation.1 | async-start | bytes 3244032 | tf_op jit(solution)/shard_map/reduce_scatter | solution.py:56
  107.0 2.0 copy-start.1
  180.7 52.3 %copy-start.2 = (f32[96]{0:T(128)}, f32[96]{0:T(128)S(1)}, u32[]{:S(2)}) copy-start(f32[96]{0:T(128)S(1)} %dynamic-slice) | copy-start | bytes 1156
Sparse Core Ops, SparseCore 0:
  130.5 100.8 reduce-scatter.1
where the time goes:
time: 240 us
  blocking collectives  119 us (50%)
  waiting for transfers between devices  50.1 us (21%)
  local copies, waits for them, and re-layouts  26.3 us (11%)
  other arithmetic  25.9 us (11%)
  between operations  14.2 us (6%)
  matrix products  4.27 us (2%)
    psum x1, blocking collectives, pick_rows(): return lax.psum(picked, ('dp', 'sub')).astype(jnp.bfloat16)  80.7 us
    reduce_scatter x1, waiting for transfers between devices, on_device(): lax.psum_scatter(placed_sums, ('dp', 'sub'), scatter_dimension=0, tiled=T...  50.1 us
    unnamed x1, blocking collectives  38.4 us
    scatter x1, other arithmetic, on_device(): jnp.zeros((total_rows, width_dim), jnp.float32).at[owner_slot]  17.1 us
    gather x1, local copies, waits for them, and re-layouts, pick_rows(): points[local_row].astype(jnp.float32)  13 us
    scatter x1, local copies, waits for them, and re-layouts, on_device(): jnp.zeros((total_rows,), jnp.float32).at[owner_slot].set(partial_mass)  11.8 us
  transfers between devices with their start and end apart: 1, of which 1 were waited for; matrix products, arithmetic and copies ran while one was open for 5% of the time, Pallas kernels for 0%

commit v1 on v0

v1 whole, which is shorter than its diff:
```python
import functools

import jax
import jax.numpy as jnp
from jax import lax
from jax.experimental import pallas as pl
from jax.experimental.pallas import tpu as pltpu
from jax.sharding import PartitionSpec as P


AXES = ("dp", "sub")
FAR = 3e38
LANES = 128
GRANT = 16 << 20


def pick_rows(round_rows, points, my_device):
    row_count = points.shape[0]
    flat_rows = round_rows.reshape(-1)
    owner_dev = flat_rows // row_count
    local_row = flat_rows % row_count
    mine = owner_dev == my_device
    picked = jnp.where(
        mine[:, None], points[local_row].astype(jnp.float32), jnp.zeros((), jnp.float32)
    )
    return lax.psum(picked, AXES).astype(jnp.bfloat16)


def any_mesh(points, candidates, owner_slot):
    cand = jnp.zeros((owner_slot.shape[0],), jnp.int32).at[owner_slot].set(candidates.reshape(-1))
    chosen = pick_rows(cand, points, lax.axis_index(AXES))
    point_norm = jnp.sum(points.astype(jnp.float32) ** 2, axis=1)
    cand_norm = jnp.sum(chosen.astype(jnp.float32) ** 2, axis=1)
    dots = lax.dot_general(
        points, chosen, (((1,), (1,)), ((), ())), preferred_element_type=jnp.float32
    )
    dist = point_norm[:, None] + cand_norm[None, :] - 2.0 * dots
    nearest = jnp.min(dist, axis=1)
    kernel = jnp.exp(-dist / 0.25).astype(jnp.bfloat16)
    sums = lax.dot_general(
        kernel, points, (((0,), (0,)), ((), ())), preferred_element_type=jnp.float32
    )
    mass = jnp.sum(kernel.astype(jnp.float32), axis=0)
    summed = lax.psum_scatter(sums, AXES, scatter_dimension=0, tiled=True)
    masses = lax.psum_scatter(mass, AXES, scatter_dimension=0, tiled=True)
    return summed / masses[:, None], masses, nearest


def send(x, chips, target):
    pairs = [(d * 2 + c, target(d, c)) for d in range(chips) for c in range(2)]
    return lax.ppermute(x, AXES, pairs)


LAST = (((1,), (1,)), ((), ()))


def column_sums(x):
    square = x * x
    high = square.astype(jnp.bfloat16)
    low = (square - high.astype(jnp.float32)).astype(jnp.bfloat16)
    ones = jnp.ones((8, x.shape[1]), jnp.bfloat16)
    return lax.dot_general(ones, high, LAST, preferred_element_type=jnp.float32) + lax.dot_general(
        ones, low, LAST, preferred_element_type=jnp.float32
    )


def scan_kernel(places, first, base_ref, cand_ref, bias_ref, own_ref, sib_ref, *refs):
    n = len(places)
    block_refs, refs = refs[:n], refs[n:]
    rows, dim = own_ref.shape
    wanted = cand_ref.shape[0]
    if first:
        sel_out, near_out, norm_out = refs
        norm_out[...] = column_sums(own_ref[...].astype(jnp.float32))
        sel = jnp.zeros((wanted, dim), jnp.float32)
        nears = [jnp.full((8, rows), FAR, jnp.float32)] * 2
    else:
        sel_in, near_in, sel_out, near_out = refs
        sel = sel_in[...].astype(jnp.float32)
        nears = [near_in[:, :rows], near_in[:, rows:]]
    lane = lax.broadcasted_iota(jnp.int32, (LANES, LANES), 1)
    spot = lax.broadcasted_iota(jnp.int32, (wanted, rows), 1)
    for place, ref in zip(places, block_refs):
        base = base_ref[place]
        block = ref[...]
        hot = (spot + base == cand_ref[...]).astype(jnp.bfloat16)
        sel += jnp.dot(hot, block, preferred_element_type=jnp.float32)
        cols = []
        for i in range(rows // LANES):
            piece = block[i * LANES : (i + 1) * LANES, :].astype(jnp.float32)
            square = piece * piece
            folded = jnp.where(lane == base // LANES + i, bias_ref[...], 0.0)
            for w in range(dim // LANES):
                folded += square[:, w * LANES : (w + 1) * LANES]
            cols.append(jnp.sum(folded, axis=1, keepdims=True))
        col = jnp.concatenate(cols, axis=0)
        twice = block * jnp.bfloat16(-2.0)
        for h, mine in enumerate((own_ref, sib_ref)):
            dots = lax.dot_general(twice, mine[...], LAST, preferred_element_type=jnp.float32)
            part = jnp.min((dots + col).reshape(rows // 8, 8, rows), axis=0)
            nears[h] = jnp.minimum(nears[h], part)
    sel_out[...] = sel.astype(sel_out.dtype)
    near_out[:, :rows] = nears[0]
    near_out[:, rows:] = nears[1]


def sum_kernel(sel_ref, got_ref, near_ref, *refs):
    block_refs, (mine_ref, theirs_ref) = refs[:-2], refs[-2:]
    wanted, dim = sel_ref.shape
    half = wanted // 2
    rows = near_ref.shape[1] // 2
    got = got_ref[...].astype(jnp.float32)
    chosen32 = sel_ref[...].astype(jnp.float32) + jnp.concatenate([got[half:], got[:half]], axis=0)
    chosen = chosen32.astype(jnp.bfloat16)
    cand_norm = column_sums(chosen32)[:1]
    sums = jnp.zeros((wanted, dim), jnp.float32)
    mass = jnp.zeros((8, wanted), jnp.float32)
    for ref in block_refs:
        block = ref[...]
        wide = block.astype(jnp.float32)
        norm = jnp.sum(wide * wide, axis=1, keepdims=True)
        dots = lax.dot_general(block, chosen, LAST, preferred_element_type=jnp.float32)
        dist = (norm + cand_norm) - 2.0 * dots
        kern = jnp.exp(dist * -4.0).astype(jnp.bfloat16)
        mass += jnp.sum(kern.astype(jnp.float32).reshape(rows // 8, 8, wanted), axis=0)
        sums += lax.dot_general(
            kern, block, (((0,), (0,)), ((), ())), preferred_element_type=jnp.float32
        )
    spare = jnp.zeros((LANES - 8, wanted), jnp.float32)
    mass = jnp.sum(jnp.concatenate([mass, spare], axis=0).T, axis=1, keepdims=True)
    near = jnp.min(near_ref[...], axis=0, keepdims=True)
    for h, ref in enumerate((mine_ref, theirs_ref)):
        ref[:half, :dim] = sums[h * half : (h + 1) * half]
        ref[:half, dim:] = jnp.broadcast_to(mass[h * half : (h + 1) * half], (half, LANES))
        wide = ref.shape[1]
        for w in range(-(-rows // wide)):
            piece = near[:, h * rows + w * wide : h * rows + min(rows, (w + 1) * wide)]
            ref[half + w : half + w + 1, : piece.shape[1]] = piece


def finish_kernel(mine_ref, back_ref, norm_ref, centroids_ref, masses_ref, nearest_ref):
    half, dim = centroids_ref.shape
    rows = nearest_ref.shape[1]
    wide = mine_ref.shape[1]
    mass = mine_ref[:half, dim:] + back_ref[:half, dim:]
    for w in range(dim // LANES):
        at = slice(w * LANES, (w + 1) * LANES)
        centroids_ref[:, at] = (mine_ref[:half, at] + back_ref[:half, at]) / mass
    spare = jnp.zeros((LANES - half, LANES), jnp.float32)
    masses_ref[...] = jnp.concatenate([mass, spare], axis=0).T[:1, :half]
    for w in range(-(-rows // wide)):
        at = slice(w * wide, min(rows, (w + 1) * wide))
        span = at.stop - at.start
        nearest = jnp.minimum(
            mine_ref[half + w : half + w + 1, :span], back_ref[half + w : half + w + 1, :span]
        )
        nearest_ref[:, at] = norm_ref[:1, at] + nearest


SENDS = {
    "sib": (None, "other"),
    "z2": ("own", "two"),
    "z1": ("own", "one"),
    "a0": ("own", "near"),
    "b0": ("own", "far"),
    "e0": ("a0", "far"),
    "a1": ("z1", "near"),
    "b1": ("z1", "far"),
    "e1": ("a1", "far"),
    "z3": ("z2", "one"),
    "a2": ("z2", "near"),
    "b2": ("z2", "far"),
    "e2": ("a2", "far"),
    "a3": ("z3", "near"),
    "b3": ("z3", "far"),
    "e3": ("a3", "far"),
}
ORDER = ("sib", "z2", "z1", "a0", "b0", "s0", "e0", "a1", "b1", "z3", "a2", "b2", "s1", "e1", "s2", "a3", "b3", "s3", "e2", "s4", "e3", "s5", "s6")
SCANS = {
    "s0": ("own",),
    "s1": ("a0", "b0", "z1"),
    "s2": ("e0", "z2"),
    "s3": ("a1", "b1", "e1", "z3"),
    "s4": ("a2", "b2"),
    "s5": ("a3", "b3", "e2"),
    "s6": ("e3",),
}
BLOCKS = sum(SCANS.values(), ())


def gathered(chips, points, candidates, owner_slot):
    rows, dim = points.shape
    total = owner_slot.shape[0]
    half = total // (2 * chips)
    d = lax.axis_index("dp")
    c = lax.axis_index("sub")
    near_bit = jnp.where(c == 0, 1, 2)
    far_bit = 3 - near_bit
    targets = {
        "other": lambda d, c: d * 2 + 1 - c,
        "one": lambda d, c: (d ^ 4) * 2 + c,
        "two": lambda d, c: (d ^ 8) * 2 + c,
        "near": lambda d, c: (d ^ (1 if c == 0 else 2)) * 2 + c,
        "far": lambda d, c: (d ^ (2 if c == 0 else 1)) * 2 + c,
    }
    steps = {"one": 4, "two": 8, "near": near_bit, "far": far_bit}

    flat = candidates.reshape(-1)
    order = jnp.arange(2 * half, dtype=jnp.int32)
    slot = jnp.where(order < half, (2 * d + c) * half + order, (2 * d + 1 - c) * half + order - half)
    cand = jnp.sum(
        jnp.where(owner_slot[None, :] == slot[:, None], flat[None, :], 0), axis=1, keepdims=True
    )
    span = 2 * chips * rows // LANES
    low = (flat[None, :] % LANES == jnp.arange(LANES, dtype=jnp.int32)[:, None]).astype(jnp.bfloat16)
    high = (flat[None, :] // LANES == jnp.arange(span, dtype=jnp.int32)[:, None]).astype(jnp.bfloat16)
    hits = lax.dot_general(low, high, LAST, preferred_element_type=jnp.float32)
    bias = jnp.where(hits > 0, 0.0, FAR).astype(jnp.float32)
    origin = {"own": d}
    for name, (source, way) in SENDS.items():
        if source:
            origin[name] = origin[source] ^ steps[way]
    base = (jnp.stack([origin[name] for name in BLOCKS]) * 2 + c).astype(jnp.int32) * rows

    smem = pl.BlockSpec(memory_space=pltpu.SMEM)
    vmem = pl.BlockSpec(memory_space=pltpu.VMEM)
    grant = pltpu.CompilerParams(vmem_limit_bytes=GRANT)
    sel_shape = jax.ShapeDtypeStruct((2 * half, dim), jnp.bfloat16)
    near_shape = jax.ShapeDtypeStruct((8, 2 * rows), jnp.float32)
    norm_shape = jax.ShapeDtypeStruct((8, rows), jnp.float32)
    blocks = {"own": points}
    sel = near = norm = None
    for name in ORDER:
        if name in SENDS:
            source, way = SENDS[name]
            blocks[name] = send(blocks[source or "own"], chips, targets[way])
            continue
        names = SCANS[name]
        work = len(names) * rows
        first = sel is None
        shapes = (sel_shape, near_shape) + ((norm_shape,) if first else ())
        carried = () if first else (sel, near)
        sel, near, *rest = pl.pallas_call(
            functools.partial(scan_kernel, [BLOCKS.index(b) for b in names], first),
            out_shape=shapes,
            in_specs=[smem] + [vmem] * (4 + len(names) + len(carried)),
            out_specs=(vmem,) * len(shapes),
            cost_estimate=pl.CostEstimate(
                flops=4 * work * dim * (rows + half), bytes_accessed=work * dim, transcendentals=0
            ),
            compiler_params=grant,
            name="scan_rows",
        )(base, cand, bias, points, blocks["sib"], *[blocks[b] for b in names], *carried)
        norm = rest[0] if first else norm

    got = send(sel, chips, targets["other"])
    deep = -(-(half + -(-rows // (dim + LANES))) // 8) * 8
    work = len(BLOCKS) * rows
    mine, theirs = pl.pallas_call(
        sum_kernel,
        out_shape=(jax.ShapeDtypeStruct((deep, dim + LANES), jnp.float32),) * 2,
        in_specs=[vmem] * (3 + len(BLOCKS)),
        out_specs=(vmem, vmem),
        cost_estimate=pl.CostEstimate(
            flops=8 * work * dim * half, bytes_accessed=work * dim * 2, transcendentals=work * 2 * half
        ),
        compiler_params=grant,
        name="sum_rows",
    )(sel, got, near, *[blocks[b] for b in BLOCKS])
    back = send(theirs, chips, targets["other"])
    centroids, masses, nearest = pl.pallas_call(
        finish_kernel,
        out_shape=(
            jax.ShapeDtypeStruct((half, dim), jnp.float32),
            jax.ShapeDtypeStruct((1, half), jnp.float32),
            jax.ShapeDtypeStruct((1, rows), jnp.float32),
        ),
        in_specs=[vmem] * 3,
        out_specs=(vmem,) * 3,
        compiler_params=grant,
        name="finish_rows",
    )(mine, back, norm)
    return centroids, masses.reshape(half), nearest.reshape(rows)


def fits(chips, cores, rows, dim, total):
    return (
        cores == 2
        and chips == 16
        and rows % LANES == 0
        and dim % LANES == 0
        and total % (16 * chips) == 0
        and total // (2 * chips) <= LANES
        and 2 * chips * rows <= LANES * LANES
    )


def on_device(chips, cores, points, candidates, owner_slot):
    if fits(chips, cores, *points.shape, owner_slot.shape[0]):
        return gathered(chips, points, candidates, owner_slot)
    return any_mesh(points, candidates, owner_slot)


def solution(mesh):
    chips, cores = mesh.shape["dp"], mesh.shape["sub"]
    placed = (P(AXES, None), P(), P())
    return jax.shard_map(
        functools.partial(on_device, chips, cores),
        mesh=mesh,
        in_specs=placed,
        out_specs=(P(AXES, None), P(AXES), P(AXES)),
        check_vma=False,
    )
```

time: 240 us -> 58.3 us (0.24)
  blocking collectives: 119 us -> 0 us
  waiting for transfers between devices: 50.1 us -> 19 us
  other arithmetic: 25.9 us -> 0.41 us
  local copies, waits for them, and re-layouts: 26.3 us -> 1.78 us
  starting transfers between devices: 0.04 us -> 19.2 us
  Pallas kernels: 0 us -> 15.8 us
  between operations: 14.2 us -> 0.77 us
  matrix products: 4.27 us -> 1.19 us
    psum x1 -> x0, blocking collectives: 80.7 us -> none  [pick_rows(): return lax.psum(picked, ('dp', 'sub')).astype(jnp.bfloat16)]
    reduce_scatter x1 -> x0, waiting for transfers between devices: 50.1 us -> none  [on_device(): lax.psum_scatter(placed_sums, ('dp', 'sub'), scatter_dimension=0, tiled=T...]
    unnamed x1 -> x0, blocking collectives: 38.4 us -> none
    ppermute x0 -> x18, starting transfers between devices: none -> 19.2 us  [send(): return lax.ppermute(x, AXES, pairs)]
    ppermute x0 -> x18, waiting for transfers between devices: none -> 19 us  [send(): return lax.ppermute(x, AXES, pairs)]
    scatter x1 -> x0, other arithmetic: 17.1 us -> none  [on_device(): jnp.zeros((total_rows, width_dim), jnp.float32).at[owner_slot]]
    pallas_call x0 -> x9, Pallas kernels: none -> 15.8 us  [the longest x7 11 us: gathered(): pl.pallas_call(functools.partial(scan_kernel, [BLOCKS.index(b) for b in n...]
    gather x1 -> x0, local copies, waits for them, and re-layouts: 13 us -> none  [pick_rows(): points[local_row].astype(jnp.float32)]
  transfers between devices with their start and end apart: 1 -> 18, of which waited for: 1 -> 8; matrix products, arithmetic and copies ran while one was open for 5% -> 4% of each run, Pallas kernels for 0% -> 17%
where the time goes in v1:
time: 58.3 us; the launch traced here: 58.1 us
  starting transfers between devices  19.2 us (33%)
  waiting for transfers between devices  19 us (33%)
  Pallas kernels  15.8 us (27%)
  local copies, waits for them, and re-layouts  1.78 us (3%)
  matrix products  1.19 us (2%)
  between operations  0.77 us (1%)
    ppermute x18, starting transfers between devices, send(): return lax.ppermute(x, AXES, pairs)  19.2 us
    ppermute x18, waiting for transfers between devices, send(): return lax.ppermute(x, AXES, pairs)  19 us
    pallas_call x7, Pallas kernels, gathered(): pl.pallas_call(functools.partial(scan_kernel, [BLOCKS.index(b) for b in n...  11 us
    pallas_call x1, Pallas kernels, gathered(): pl.pallas_call(sum_kernel, out_shape=(jax.ShapeDtypeStruct((deep, dim + L...  4.05 us
    dot_general x1, matrix products, gathered(): hits = lax.dot_general(low, high, LAST, preferred_element_type=jnp.float32)  1.19 us
  transfers between devices with their start and end apart: 18, of which 8 were waited for; matrix products, arithmetic and copies ran while one was open for 4% of the time, Pallas kernels for 17%

profile of v1, /device:TPU:0, one launch (start us, length us, event | category | flops | bytes accessed | tf_op | source)
XLA Modules:
  0.0 58.1 jit_solution(14208060973130130202)
XLA Ops:
  0.6 3.1 %collective-permute-start.15 = (bf16[512,256]{1,0:T(8,128)(2,1)}, bf16[512,256]{1,0:T(8,128)(2,1)S(1)}, u32[]{:S(2)}, u32[]{:S(2)}) collective-permute-start(bf16[512,256]{1,0:T(8,128)(2,1)} %refs_0_.3), channel_id=1, source_target_pairs={{0,4},{1,3},{2,6},{3,1},{4,0},{5,7},{6,2},{7,5},{8,12},{9,11},{10,... | collective-permute-start | bytes 786440 | tf_op jit(solution)/shard_map/ppermute | solution.py:51
  3.7 1.5 %collective-permute-start.13 = (bf16[512,256]{1,0:T(8,128)(2,1)}, bf16[512,256]{1,0:T(8,128)(2,1)S(1)}, u32[]{:S(2)}, u32[]{:S(2)}) collective-permute-start(bf16[512,256]{1,0:T(8,128)(2,1)} %refs_0_.3), channel_id=1, source_target_pairs={{0,2},{1,5},{2,0},{3,7},{4,6},{5,1},{6,4},{7,3},{8,10},{9,13},{10,... | collective-permute-start | bytes 786440 | tf_op jit(solution)/shard_map/ppermute | solution.py:51
  5.2 1.6 %collective-permute-start.9 = (bf16[512,256]{1,0:T(8,128)(2,1)}, bf16[512,256]{1,0:T(8,128)(2,1)S(1)}, u32[]{:S(2)}, u32[]{:S(2)}) collective-permute-start(bf16[512,256]{1,0:T(8,128)(2,1)} %refs_0_.3), channel_id=1, source_target_pairs={{0,8},{1,9},{2,10},{3,11},{4,12},{5,13},{6,14},{7,15},{8,0},{9,1},... | collective-permute-start | bytes 786440 | tf_op jit(solution)/shard_map/ppermute | solution.py:51
  6.8 2.6 %collective-permute-start.1 = (bf16[512,256]{1,0:T(8,128)(2,1)}, bf16[512,256]{1,0:T(8,128)(2,1)S(1)}, u32[]{:S(2)}, u32[]{:S(2)}) collective-permute-start(bf16[512,256]{1,0:T(8,128)(2,1)} %refs_0_.3), channel_id=1, source_target_pairs={{0,16},{1,17},{2,18},{3,19},{4,20},{5,21},{6,22},{7,23},{8,24},{9,... | collective-permute-start | bytes 786440 | tf_op jit(solution)/shard_map/ppermute | solution.py:51
  9.4 0.7 %broadcast_in_dim.27 = s32[3072]{0:T(1024)S(1)} reshape(s32[4,768]{1,0:T(4,128)} %param.4) | data formatting | bytes 24576 | tf_op jit(solution)/shard_map/jit(_where)/broadcast_in_dim | solution.py:212
  10.1 1.2 %fusion.2.bias_ref = f32[128,128]{1,0:T(8,128)} fusion(s32[3072]{0:T(1024)S(1)} %get-tuple-element.44, s32[3072]{0:T(1024)S(1)} %get-tuple-element.43), kind=kOutput, calls=%fused_computation.5 | convolution fusion | flops 101482496 | bytes 90112 | tf_op jit(solution)/shard_map/dot_general | solution.py:217
  11.4 7.0 %collective-permute-done.9.refs_2_.refs_3_ = bf16[512,256]{1,0:T(8,128)(2,1)S(1)} collective-permute-done((bf16[512,256]{1,0:T(8,128)(2,1)}, bf16[512,256]{1,0:T(8,128)(2,1)S(1)}, u32[]{:S(2)}, u32[]{:S(2)}) %collective-permute-start.9) | collective-permute-done | bytes 262176 | tf_op jit(solution)/shard_map/ppermute | solution.py:51
  18.4 0.5 collective-permute-start.10
  18.9 2.0 %collective-permute-done.1.refs_1_.refs_5_ = bf16[512,256]{1,0:T(8,128)(2,1)S(1)} collective-permute-done((bf16[512,256]{1,0:T(8,128)(2,1)}, bf16[512,256]{1,0:T(8,128)(2,1)S(1)}, u32[]{:S(2)}, u32[]{:S(2)}) %collective-permute-start.1) | collective-permute-done | bytes 262176 | tf_op jit(solution)/shard_map/ppermute | solution.py:51
  21.2 0.5 collective-permute-start.11
  21.7 0.5 collective-permute-start.6
  22.2 1.5 %collective-permute-start.14 = (bf16[512,256]{1,0:T(8,128)(2,1)S(1)}, bf16[512,256]{1,0:T(8,128)(2,1)S(1)}, u32[]{:S(2)}, u32[]{:S(2)}) collective-permute-start(bf16[512,256]{1,0:T(8,128)(2,1)S(1)} %collective-permute-done.13.refs_0_.refs_1_), channel_id=1, source_target_pairs={{0,4},{1,3},{2,6},{3,1},{4,0},{5,7},{6,2},{7,5},{8,12},{9,11},{10,... | collective-permute-start | bytes 786440 | tf_op jit(solution)/shard_map/ppermute | solution.py:51
  23.8 3.8 %collective-permute-done.10.refs_0_.refs_6_ = bf16[512,256]{1,0:T(8,128)(2,1)S(1)} collective-permute-done((bf16[512,256]{1,0:T(8,128)(2,1)S(1)}, bf16[512,256]{1,0:T(8,128)(2,1)S(1)}, u32[]{:S(2)}, u32[]{:S(2)}) %collective-permute-start.10) | collective-permute-done | bytes 262176 | tf_op jit(solution)/shard_map/ppermute | solution.py:51
  27.5 0.5 collective-permute-start.12
  28.9 0.8 %copy-done.1 = f32[128,128]{1,0:T(8,128)S(1)} copy-done((f32[128,128]{1,0:T(8,128)S(1)}, f32[128,128]{1,0:T(8,128)}, u32[]{:S(2)}) %copy-start.1) | copy-done | bytes 65560
  29.8 1.3 %scan_rows.7 = (bf16[192,256]{1,0:T(8,128)(2,1)S(1)}, f32[8,1024]{1,0:T(8,128)S(1)}, f32[8,512]{1,0:T(8,128)S(1)}) custom-call(s32[16]{0:T(128)S(1)} %add_multiply_fusion.base_ref, s32[192,1]{1,0:T(8,128)S(1)} %copy.19.cand_ref, f32[128,128]{1,0:T(8,128)S(1)} %copy-done.1, bf16[512,256]{1,0:T(8,128)(2,1)S(1)} %copy-done, ...), custom_call_target="tpu_custom_call" | custom-call | flops 318767104 | bytes 131072 | tf_op jit(solution)/shard_map/scan_rows/pallas_call | solution.py:243
  31.0 2.4 %collective-permute-done.14.refs_0_.refs_4_ = bf16[512,256]{1,0:T(8,128)(2,1)S(1)} collective-permute-done((bf16[512,256]{1,0:T(8,128)(2,1)S(1)}, bf16[512,256]{1,0:T(8,128)(2,1)S(1)}, u32[]{:S(2)}, u32[]{:S(2)}) %collective-permute-start.14) | collective-permute-done | bytes 262176 | tf_op jit(solution)/shard_map/ppermute | solution.py:51
  33.9 1.5 %collective-permute-start.5 = (bf16[512,256]{1,0:T(8,128)(2,1)S(1)}, bf16[512,256]{1,0:T(8,128)(2,1)S(1)}, u32[]{:S(2)}, u32[]{:S(2)}) collective-permute-start(bf16[512,256]{1,0:T(8,128)(2,1)S(1)} %collective-permute-done.2.refs_3_.refs_9_), channel_id=1, source_target_pairs={{0,4},{1,3},{2,6},{3,1},{4,0},{5,7},{6,2},{7,5},{8,12},{9,11},{10,... | collective-permute-start | bytes 786440 | tf_op jit(solution)/shard_map/ppermute | solution.py:51
  35.9 1.8 %scan_rows.8 = (bf16[192,256]{1,0:T(8,128)(2,1)S(1)}, f32[8,1024]{1,0:T(8,128)S(1)}) custom-call(s32[16]{0:T(128)S(1)} %add_multiply_fusion.base_ref, s32[192,1]{1,0:T(8,128)S(1)} %copy.19.cand_ref, f32[128,128]{1,0:T(8,128)S(1)} %copy-done.1, bf16[512,256]{1,0:T(8,128)(2,1)S(1)} %copy-done, bf16[512,256]{1,0:T(8,128)(2,1)S(1)} %collective-permute-done.sib_ref, ...), custom_call_target="tpu_custom_call" | custom-call | flops 956301312 | bytes 393216 | tf_op jit(solution)/shard_map/scan_rows/pallas_call | solution.py:243
  37.7 1.4 %scan_rows.9 = (bf16[192,256]{1,0:T(8,128)(2,1)S(1)}, f32[8,1024]{1,0:T(8,128)S(1)}) custom-call(s32[16]{0:T(128)S(1)} %add_multiply_fusion.base_ref, s32[192,1]{1,0:T(8,128)S(1)} %copy.19.cand_ref, f32[128,128]{1,0:T(8,128)S(1)} %copy-done.1, bf16[512,256]{1,0:T(8,128)(2,1)S(1)} %copy-done, bf16[512,256]{1,0:T(8,128)(2,1)S(1)} %collective-permute-done.sib_ref, ...), custom_call_target="tpu_custom_call" | custom-call | flops 637534208 | bytes 262144 | tf_op jit(solution)/shard_map/scan_rows/pallas_call | solution.py:243
  39.2 1.6 %collective-permute-start.4 = (bf16[512,256]{1,0:T(8,128)(2,1)S(1)}, bf16[512,256]{1,0:T(8,128)(2,1)S(1)}, u32[]{:S(2)}, u32[]{:S(2)}) collective-permute-start(bf16[512,256]{1,0:T(8,128)(2,1)S(1)} %collective-permute-done.3.refs_0_.refs_12_), channel_id=1, source_target_pairs={{0,4},{1,3},{2,6},{3,1},{4,0},{5,7},{6,2},{7,5},{8,12},{9,11},{10,... | collective-permute-start | bytes 786440 | tf_op jit(solution)/shard_map/ppermute | solution.py:51
  40.8 2.2 %scan_rows.10 = (bf16[192,256]{1,0:T(8,128)(2,1)S(1)}, f32[8,1024]{1,0:T(8,128)S(1)}) custom-call(s32[16]{0:T(128)S(1)} %add_multiply_fusion.base_ref, s32[192,1]{1,0:T(8,128)S(1)} %copy.19.cand_ref, f32[128,128]{1,0:T(8,128)S(1)} %copy-done.1, bf16[512,256]{1,0:T(8,128)(2,1)S(1)} %copy-done, bf16[512,256]{1,0:T(8,128)(2,1)S(1)} %collective-permute-done.sib_ref, ...), custom_call_target="tpu_custom_call" | custom-call | flops 1275068416 | bytes 524288 | tf_op jit(solution)/shard_map/scan_rows/pallas_call | solution.py:243
  43.0 1.4 %scan_rows.11 = (bf16[192,256]{1,0:T(8,128)(2,1)S(1)}, f32[8,1024]{1,0:T(8,128)S(1)}) custom-call(s32[16]{0:T(128)S(1)} %add_multiply_fusion.base_ref, s32[192,1]{1,0:T(8,128)S(1)} %copy.19.cand_ref, f32[128,128]{1,0:T(8,128)S(1)} %copy-done.1, bf16[512,256]{1,0:T(8,128)(2,1)S(1)} %copy-done, bf16[512,256]{1,0:T(8,128)(2,1)S(1)} %collective-permute-done.sib_ref, ...), custom_call_target="tpu_custom_call" | custom-call | flops 637534208 | bytes 262144 | tf_op jit(solution)/shard_map/scan_rows/pallas_call | solution.py:243
  44.4 0.9 %collective-permute-done.7.refs_2_.refs_14_ = bf16[512,256]{1,0:T(8,128)(2,1)S(1)} collective-permute-done((bf16[512,256]{1,0:T(8,128)(2,1)S(1)}, bf16[512,256]{1,0:T(8,128)(2,1)S(1)}, u32[]{:S(2)}, u32[]{:S(2)}) %collective-permute-start.7) | collective-permute-done | bytes 262176 | tf_op jit(solution)/shard_map/ppermute | solution.py:51
  45.4 1.8 %scan_rows.12 = (bf16[192,256]{1,0:T(8,128)(2,1)S(1)}, f32[8,1024]{1,0:T(8,128)S(1)}) custom-call(s32[16]{0:T(128)S(1)} %add_multiply_fusion.base_ref, s32[192,1]{1,0:T(8,128)S(1)} %copy.19.cand_ref, f32[128,128]{1,0:T(8,128)S(1)} %copy-done.1, bf16[512,256]{1,0:T(8,128)(2,1)S(1)} %copy-done, bf16[512,256]{1,0:T(8,128)(2,1)S(1)} %collective-permute-done.sib_ref, ...), custom_call_target="tpu_custom_call" | custom-call | flops 956301312 | bytes 393216 | tf_op jit(solution)/shard_map/scan_rows/pallas_call | solution.py:243
  47.2 1.0 %collective-permute-done.4.refs_0_.refs_15_ = bf16[512,256]{1,0:T(8,128)(2,1)S(1)} collective-permute-done((bf16[512,256]{1,0:T(8,128)(2,1)S(1)}, bf16[512,256]{1,0:T(8,128)(2,1)S(1)}, u32[]{:S(2)}, u32[]{:S(2)}) %collective-permute-start.4) | collective-permute-done | bytes 262176 | tf_op jit(solution)/shard_map/ppermute | solution.py:51
  48.2 1.1 %scan_rows.13 = (bf16[192,256]{1,0:T(8,128)(2,1)S(1)}, f32[8,1024]{1,0:T(8,128)S(1)}) custom-call(s32[16]{0:T(128)S(1)} %add_multiply_fusion.base_ref, s32[192,1]{1,0:T(8,128)S(1)} %copy.19.cand_ref, f32[128,128]{1,0:T(8,128)S(1)} %copy-done.2, bf16[512,256]{1,0:T(8,128)(2,1)S(1)} %copy-done, bf16[512,256]{1,0:T(8,128)(2,1)S(1)} %collective-permute-done.sib_ref, ...), custom_call_target="tpu_custom_call" | custom-call | flops 318767104 | bytes 131072 | tf_op jit(solution)/shard_map/scan_rows/pallas_call | solution.py:243
  49.3 1.7 %collective-permute-start.16 = (bf16[192,256]{1,0:T(8,128)(2,1)S(1)}, bf16[192,256]{1,0:T(8,128)(2,1)S(1)}, u32[]{:S(2)}, u32[]{:S(2)}) collective-permute-start(bf16[192,256]{1,0:T(8,128)(2,1)S(1)} %get-tuple-element.35.sel_ref), channel_id=1, source_target_pairs={{0,1},{1,0},{2,3},{3,2},{4,5},{5,4},{6,7},{7,6},{8,9},{9,8},{10,11... | collective-permute-start | bytes 294920 | tf_op jit(solution)/shard_map/ppermute | solution.py:51
  51.0 0.9 %collective-permute-done.16.got_ref = bf16[192,256]{1,0:T(8,128)(2,1)S(1)} collective-permute-done((bf16[192,256]{1,0:T(8,128)(2,1)S(1)}, bf16[192,256]{1,0:T(8,128)(2,1)S(1)}, u32[]{:S(2)}, u32[]{:S(2)}) %collective-permute-start.16) | collective-permute-done | bytes 98336 | tf_op jit(solution)/shard_map/ppermute | solution.py:51
  51.9 4.0 %sum_rows.1 = (f32[104,384]{1,0:T(8,128)S(1)}, f32[104,384]{1,0:T(8,128)S(1)}) custom-call(bf16[192,256]{1,0:T(8,128)(2,1)S(1)} %get-tuple-element.35.sel_ref, bf16[192,256]{1,0:T(8,128)(2,1)S(1)} %collective-permute-done.16.got_ref, f32[8,1024]{1,0:T(8,128)S(1)} %get-tuple-element.36.near_ref, bf16[512,256]{1,0:T(8,128)(2,1)S(1)} %copy-done, ...), custom_call_target="tpu_custom_call" | custom-call | flops 1610612736 | bytes 4194304 | tf_op jit(solution)/shard_map/sum_rows/pallas_call | solution.py:259
  56.4 1.0 %collective-permute-done.17.back_ref = f32[104,384]{1,0:T(8,128)S(1)} collective-permute-done((f32[104,384]{1,0:T(8,128)S(1)}, f32[104,384]{1,0:T(8,128)S(1)}, u32[]{:S(2)}, u32[]{:S(2)}) %collective-permute-start.17) | collective-permute-done | bytes 159776 | tf_op jit(solution)/shard_map/ppermute | solution.py:51
  57.4 0.7 %finish_rows.1 = (f32[96,256]{1,0:T(8,128)}, f32[1,96]{1,0:T(1,128)}, f32[1,512]{1,0:T(1,128)}) custom-call(f32[104,384]{1,0:T(8,128)S(1)} %get-tuple-element.37.mine_ref, f32[104,384]{1,0:T(8,128)S(1)} %collective-permute-done.17.back_ref, f32[8,512]{1,0:T(8,128)S(1)} %get-tuple-element.39.norm_ref), custom_call_target="tpu_custom_call" | custom-call | tf_op jit(solution)/shard_map/finish_rows/pallas_call | solution.py:271
  (29 shorter events, 2.8 us)
Async XLA Ops:
  0.6 20.6 %collective-permute-start.15 = (bf16[512,256]{1,0:T(8,128)(2,1)}, bf16[512,256]{1,0:T(8,128)(2,1)S(1)}, u32[]{:S(2)}, u32[]{:S(2)}) collective-permute-start(bf16[512,256]{1,0:T(8,128)(2,1)} %refs_0_.3), channel_id=1, source_target_pairs={{0,4},{1,3},{2,6},{3,1},{4,0},{5,7},{6,2},{7,5},{8,12},{9,11},{10,... | collective-permute-start | bytes 786440 | tf_op jit(solution)/shard_map/ppermute | solution.py:51
  3.7 18.0 %collective-permute-start.13 = (bf16[512,256]{1,0:T(8,128)(2,1)}, bf16[512,256]{1,0:T(8,128)(2,1)S(1)}, u32[]{:S(2)}, u32[]{:S(2)}) collective-permute-start(bf16[512,256]{1,0:T(8,128)(2,1)} %refs_0_.3), channel_id=1, source_target_pairs={{0,2},{1,5},{2,0},{3,7},{4,6},{5,1},{6,4},{7,3},{8,10},{9,13},{10,... | collective-permute-start | bytes 786440 | tf_op jit(solution)/shard_map/ppermute | solution.py:51
  5.2 13.2 %collective-permute-start.9 = (bf16[512,256]{1,0:T(8,128)(2,1)}, bf16[512,256]{1,0:T(8,128)(2,1)S(1)}, u32[]{:S(2)}, u32[]{:S(2)}) collective-permute-start(bf16[512,256]{1,0:T(8,128)(2,1)} %refs_0_.3), channel_id=1, source_target_pairs={{0,8},{1,9},{2,10},{3,11},{4,12},{5,13},{6,14},{7,15},{8,0},{9,1},... | collective-permute-start | bytes 786440 | tf_op jit(solution)/shard_map/ppermute | solution.py:51
  6.8 14.1 %collective-permute-start.1 = (bf16[512,256]{1,0:T(8,128)(2,1)}, bf16[512,256]{1,0:T(8,128)(2,1)S(1)}, u32[]{:S(2)}, u32[]{:S(2)}) collective-permute-start(bf16[512,256]{1,0:T(8,128)(2,1)} %refs_0_.3), channel_id=1, source_target_pairs={{0,16},{1,17},{2,18},{3,19},{4,20},{5,21},{6,22},{7,23},{8,24},{9,... | collective-permute-start | bytes 786440 | tf_op jit(solution)/shard_map/ppermute | solution.py:51
  9.3 12.9 %collective-permute-start = (bf16[512,256]{1,0:T(8,128)(2,1)}, bf16[512,256]{1,0:T(8,128)(2,1)S(1)}, u32[]{:S(2)}, u32[]{:S(2)}) collective-permute-start(bf16[512,256]{1,0:T(8,128)(2,1)} %refs_0_.3), channel_id=1, source_target_pairs={{0,1},{1,0},{2,3},{3,2},{4,5},{5,4},{6,7},{7,6},{8,9},{9,8},{10,11... | collective-permute-start | bytes 786440 | tf_op jit(solution)/shard_map/ppermute | solution.py:51
  10.1 18.3 %copy-start.3 = (s32[3072]{0:T(1024)S(1)}, s32[3072]{0:T(1024)}, u32[]{:S(2)}) copy-start(s32[3072]{0:T(1024)} %param.5) | copy-start | bytes 36868
  10.1 18.8 %copy-start = (bf16[512,256]{1,0:T(8,128)(2,1)S(1)}, bf16[512,256]{1,0:T(8,128)(2,1)}, u32[]{:S(2)}) copy-start(bf16[512,256]{1,0:T(8,128)(2,1)} %refs_0_.3) | copy-start | bytes 786436
  18.4 9.2 %collective-permute-start.10 = (bf16[512,256]{1,0:T(8,128)(2,1)S(1)}, bf16[512,256]{1,0:T(8,128)(2,1)S(1)}, u32[]{:S(2)}, u32[]{:S(2)}) collective-permute-start(bf16[512,256]{1,0:T(8,128)(2,1)S(1)} %collective-permute-done.9.refs_2_.refs_3_), channel_id=1, source_target_pairs={{0,2},{1,5},{2,0},{3,7},{4,6},{5,1},{6,4},{7,3},{8,10},{9,13},{10,... | collective-permute-start | bytes 786440 | tf_op jit(solution)/shard_map/ppermute | solution.py:51
  20.9 7.2 %collective-permute-start.2 = (bf16[512,256]{1,0:T(8,128)(2,1)S(1)}, bf16[512,256]{1,0:T(8,128)(2,1)S(1)}, u32[]{:S(2)}, u32[]{:S(2)}) collective-permute-start(bf16[512,256]{1,0:T(8,128)(2,1)S(1)} %collective-permute-done.1.refs_1_.refs_5_), channel_id=1, source_target_pairs={{0,8},{1,9},{2,10},{3,11},{4,12},{5,13},{6,14},{7,15},{8,0},{9,1},... | collective-permute-start | bytes 786440 | tf_op jit(solution)/shard_map/ppermute | solution.py:51
  21.2 12.7 %collective-permute-start.11 = (bf16[512,256]{1,0:T(8,128)(2,1)S(1)}, bf16[512,256]{1,0:T(8,128)(2,1)S(1)}, u32[]{:S(2)}, u32[]{:S(2)}) collective-permute-start(bf16[512,256]{1,0:T(8,128)(2,1)S(1)} %collective-permute-done.9.refs_2_.refs_3_), channel_id=1, source_target_pairs={{0,4},{1,3},{2,6},{3,1},{4,0},{5,7},{6,2},{7,5},{8,12},{9,11},{10,... | collective-permute-start | bytes 786440 | tf_op jit(solution)/shard_map/ppermute | solution.py:51
  21.7 13.7 %collective-permute-start.6 = (bf16[512,256]{1,0:T(8,128)(2,1)S(1)}, bf16[512,256]{1,0:T(8,128)(2,1)S(1)}, u32[]{:S(2)}, u32[]{:S(2)}) collective-permute-start(bf16[512,256]{1,0:T(8,128)(2,1)S(1)} %collective-permute-done.1.refs_1_.refs_5_), channel_id=1, source_target_pairs={{0,2},{1,5},{2,0},{3,7},{4,6},{5,1},{6,4},{7,3},{8,10},{9,13},{10,... | collective-permute-start | bytes 786440 | tf_op jit(solution)/shard_map/ppermute | solution.py:51
  22.2 11.1 %collective-permute-start.14 = (bf16[512,256]{1,0:T(8,128)(2,1)S(1)}, bf16[512,256]{1,0:T(8,128)(2,1)S(1)}, u32[]{:S(2)}, u32[]{:S(2)}) collective-permute-start(bf16[512,256]{1,0:T(8,128)(2,1)S(1)} %collective-permute-done.13.refs_0_.refs_1_), channel_id=1, source_target_pairs={{0,4},{1,3},{2,6},{3,1},{4,0},{5,7},{6,2},{7,5},{8,12},{9,11},{10,... | collective-permute-start | bytes 786440 | tf_op jit(solution)/shard_map/ppermute | solution.py:51
  27.5 13.2 %collective-permute-start.12 = (bf16[512,256]{1,0:T(8,128)(2,1)S(1)}, bf16[512,256]{1,0:T(8,128)(2,1)S(1)}, u32[]{:S(2)}, u32[]{:S(2)}) collective-permute-start(bf16[512,256]{1,0:T(8,128)(2,1)S(1)} %collective-permute-done.10.refs_0_.refs_6_), channel_id=1, source_target_pairs={{0,4},{1,3},{2,6},{3,1},{4,0},{5,7},{6,2},{7,5},{8,12},{9,11},{10,... | collective-permute-start | bytes 786440 | tf_op jit(solution)/shard_map/ppermute | solution.py:51
  28.1 11.1 %collective-permute-start.3 = (bf16[512,256]{1,0:T(8,128)(2,1)S(1)}, bf16[512,256]{1,0:T(8,128)(2,1)S(1)}, u32[]{:S(2)}, u32[]{:S(2)}) collective-permute-start(bf16[512,256]{1,0:T(8,128)(2,1)S(1)} %collective-permute-done.2.refs_3_.refs_9_), channel_id=1, source_target_pairs={{0,2},{1,5},{2,0},{3,7},{4,6},{5,1},{6,4},{7,3},{8,10},{9,13},{10,... | collective-permute-start | bytes 786440 | tf_op jit(solution)/shard_map/ppermute | solution.py:51
  28.9 0.8 %copy-start.1 = (f32[128,128]{1,0:T(8,128)S(1)}, f32[128,128]{1,0:T(8,128)}, u32[]{:S(2)}) copy-start(f32[128,128]{1,0:T(8,128)} %fusion.2.bias_ref) | copy-start | bytes 196612
  33.4 9.6 %collective-permute-start.8 = (bf16[512,256]{1,0:T(8,128)(2,1)S(1)}, bf16[512,256]{1,0:T(8,128)(2,1)S(1)}, u32[]{:S(2)}, u32[]{:S(2)}) collective-permute-start(bf16[512,256]{1,0:T(8,128)(2,1)S(1)} %collective-permute-done.1.refs_1_.refs_5_), channel_id=1, source_target_pairs={{0,4},{1,3},{2,6},{3,1},{4,0},{5,7},{6,2},{7,5},{8,12},{9,11},{10,... | collective-permute-start | bytes 786440 | tf_op jit(solution)/shard_map/ppermute | solution.py:51
  33.9 11.5 %collective-permute-start.5 = (bf16[512,256]{1,0:T(8,128)(2,1)S(1)}, bf16[512,256]{1,0:T(8,128)(2,1)S(1)}, u32[]{:S(2)}, u32[]{:S(2)}) collective-permute-start(bf16[512,256]{1,0:T(8,128)(2,1)S(1)} %collective-permute-done.2.refs_3_.refs_9_), channel_id=1, source_target_pairs={{0,4},{1,3},{2,6},{3,1},{4,0},{5,7},{6,2},{7,5},{8,12},{9,11},{10,... | collective-permute-start | bytes 786440 | tf_op jit(solution)/shard_map/ppermute | solution.py:51
  35.4 10.0 %collective-permute-start.7 = (bf16[512,256]{1,0:T(8,128)(2,1)S(1)}, bf16[512,256]{1,0:T(8,128)(2,1)S(1)}, u32[]{:S(2)}, u32[]{:S(2)}) collective-permute-start(bf16[512,256]{1,0:T(8,128)(2,1)S(1)} %collective-permute-done.6.refs_0_.refs_10_), channel_id=1, source_target_pairs={{0,4},{1,3},{2,6},{3,1},{4,0},{5,7},{6,2},{7,5},{8,12},{9,11},{10,... | collective-permute-start | bytes 786440 | tf_op jit(solution)/shard_map/ppermute | solution.py:51
  39.2 9.0 %collective-permute-start.4 = (bf16[512,256]{1,0:T(8,128)(2,1)S(1)}, bf16[512,256]{1,0:T(8,128)(2,1)S(1)}, u32[]{:S(2)}, u32[]{:S(2)}) collective-permute-start(bf16[512,256]{1,0:T(8,128)(2,1)S(1)} %collective-permute-done.3.refs_0_.refs_12_), channel_id=1, source_target_pairs={{0,4},{1,3},{2,6},{3,1},{4,0},{5,7},{6,2},{7,5},{8,12},{9,11},{10,... | collective-permute-start | bytes 786440 | tf_op jit(solution)/shard_map/ppermute | solution.py:51
  45.4 2.8 %copy-start.2 = (f32[128,128]{1,0:T(8,128)S(1)}, f32[128,128]{1,0:T(8,128)}, u32[]{:S(2)}) copy-start(f32[128,128]{1,0:T(8,128)} %fusion.2.bias_ref) | copy-start | bytes 196612
  49.3 2.6 %collective-permute-start.16 = (bf16[192,256]{1,0:T(8,128)(2,1)S(1)}, bf16[192,256]{1,0:T(8,128)(2,1)S(1)}, u32[]{:S(2)}, u32[]{:S(2)}) collective-permute-start(bf16[192,256]{1,0:T(8,128)(2,1)S(1)} %get-tuple-element.35.sel_ref), channel_id=1, source_target_pairs={{0,1},{1,0},{2,3},{3,2},{4,5},{5,4},{6,7},{7,6},{8,9},{9,8},{10,11... | collective-permute-start | bytes 294920 | tf_op jit(solution)/shard_map/ppermute | solution.py:51
  56.0 1.5 %collective-permute-start.17 = (f32[104,384]{1,0:T(8,128)S(1)}, f32[104,384]{1,0:T(8,128)S(1)}, u32[]{:S(2)}, u32[]{:S(2)}) collective-permute-start(f32[104,384]{1,0:T(8,128)S(1)} %get-tuple-element.38), channel_id=1, source_target_pairs={{0,1},{1,0},{2,3},{3,2},{4,5},{5,4},{6,7},{7,6},{8,9},{9,8},{10,11... | collective-permute-start | bytes 479240 | tf_op jit(solution)/shard_map/ppermute | solution.py:51

commit v2 on v1

--- a/solution.py
+++ b/solution.py
@@ -1,4 +1,5 @@
 import functools
+import math
 
 import jax
 import jax.numpy as jnp
@@ -11,6 +12,7 @@
 AXES = ("dp", "sub")
 FAR = 3e38
 LANES = 128
+SHIFT = 7
 GRANT = 16 << 20
 
 
@@ -64,64 +66,109 @@
     )
 
 
-def scan_kernel(places, first, base_ref, cand_ref, bias_ref, own_ref, sib_ref, *refs):
+def index_kernel(meta_ref, cand_ref, owner_ref, wanted_ref, bias_ref):
+    rounds, width = cand_ref.shape
+    total = wanted_ref.shape[0]
+    place = lax.broadcasted_iota(jnp.int32, (total, 1), 0)
+    half = total // 2
+    slot = jnp.where(place < half, meta_ref[0] + place, meta_ref[1] + place - half)
+    spot = lax.broadcasted_iota(jnp.int32, (LANES, width), 0)
+    wanted = jnp.zeros((total, 1), jnp.float32)
+    hits = jnp.zeros((LANES, LANES), jnp.float32)
+    for r in range(rounds):
+        cand = cand_ref[r : r + 1, :]
+        owner = owner_ref[:, r * width : (r + 1) * width]
+        found = jnp.where(owner == slot, cand.astype(jnp.float32), 0.0)
+        wanted += jnp.sum(found, axis=1, keepdims=True)
+        low = ((cand & (LANES - 1)) == spot).astype(jnp.bfloat16)
+        high = (lax.shift_right_logical(cand, SHIFT) == spot).astype(jnp.bfloat16)
+        hits += lax.dot_general(low, high, LAST, preferred_element_type=jnp.float32)
+    wanted_ref[...] = wanted.astype(jnp.int32)
+    bias_ref[...] = jnp.where(hits > 0, 0.0, FAR)
+
+
+def pick_kernel(places, first, base_ref, cand_ref, *refs):
+    block_refs, sel_out = refs[: len(places)], refs[-1]
+    wanted, dim = sel_out.shape
+    sel = jnp.zeros((wanted, dim), jnp.float32) if first else refs[-2][...].astype(jnp.float32)
+    for place, ref in zip(places, block_refs):
+        spot = lax.broadcasted_iota(jnp.int32, (wanted, ref.shape[0]), 1)
+        hot = (spot + base_ref[place] == cand_ref[...]).astype(jnp.bfloat16)
+        sel += jnp.dot(hot, ref[...], preferred_element_type=jnp.float32)
+    sel_out[...] = sel.astype(sel_out.dtype)
+
+
+def near_kernel(places, first, base_ref, bias_ref, own_ref, sib_ref, *refs):
     n = len(places)
     block_refs, refs = refs[:n], refs[n:]
     rows, dim = own_ref.shape
-    wanted = cand_ref.shape[0]
     if first:
-        sel_out, near_out, norm_out = refs
-        norm_out[...] = column_sums(own_ref[...].astype(jnp.float32))
-        sel = jnp.zeros((wanted, dim), jnp.float32)
+        near_out, total_out, *norm_outs = refs
+        total_out[...] = column_sums(own_ref[...].astype(jnp.float32))
         nears = [jnp.full((8, rows), FAR, jnp.float32)] * 2
     else:
-        sel_in, near_in, sel_out, near_out = refs
-        sel = sel_in[...].astype(jnp.float32)
+        near_in, near_out, *norm_outs = refs
         nears = [near_in[:, :rows], near_in[:, rows:]]
     lane = lax.broadcasted_iota(jnp.int32, (LANES, LANES), 1)
-    spot = lax.broadcasted_iota(jnp.int32, (wanted, rows), 1)
-    for place, ref in zip(places, block_refs):
+    for place, ref, norm_out in zip(places, block_refs, norm_outs):
         base = base_ref[place]
         block = ref[...]
-        hot = (spot + base == cand_ref[...]).astype(jnp.bfloat16)
-        sel += jnp.dot(hot, block, preferred_element_type=jnp.float32)
         cols = []
         for i in range(rows // LANES):
             piece = block[i * LANES : (i + 1) * LANES, :].astype(jnp.float32)
             square = piece * piece
-            folded = jnp.where(lane == base // LANES + i, bias_ref[...], 0.0)
-            for w in range(dim // LANES):
+            folded = square[:, :LANES]
+            for w in range(1, dim // LANES):
                 folded += square[:, w * LANES : (w + 1) * LANES]
-            cols.append(jnp.sum(folded, axis=1, keepdims=True))
+            norm = jnp.sum(folded, axis=1, keepdims=True)
+            norm_out[i * LANES : (i + 1) * LANES, :] = jnp.broadcast_to(norm, (LANES, LANES))
+            mask = jnp.where(lane == lax.shift_right_logical(base, SHIFT) + i, bias_ref[...], 0.0)
+            cols.append(norm + jnp.sum(mask, axis=1, keepdims=True))
         col = jnp.concatenate(cols, axis=0)
         twice = block * jnp.bfloat16(-2.0)
         for h, mine in enumerate((own_ref, sib_ref)):
             dots = lax.dot_general(twice, mine[...], LAST, preferred_element_type=jnp.float32)
             part = jnp.min((dots + col).reshape(rows // 8, 8, rows), axis=0)
             nears[h] = jnp.minimum(nears[h], part)
-    sel_out[...] = sel.astype(sel_out.dtype)
     near_out[:, :rows] = nears[0]
     near_out[:, rows:] = nears[1]
 
 
+def both_kernel(places, first, base_ref, cand_ref, bias_ref, own_ref, sib_ref, *refs):
+    n = len(places)
+    blocks, refs = refs[:n], refs[n:]
+    if first:
+        sel, near = refs[:1], refs[1:]
+    else:
+        sel, near = (refs[0], refs[2]), (refs[1], *refs[3:])
+    pick_kernel(places, first, base_ref, cand_ref, *blocks, *sel)
+    near_kernel(places, first, base_ref, bias_ref, own_ref, sib_ref, *blocks, *near)
+
+
 def sum_kernel(sel_ref, got_ref, near_ref, *refs):
-    block_refs, (mine_ref, theirs_ref) = refs[:-2], refs[-2:]
+    n = (len(refs) - 2) // 2
+    block_refs, norm_refs, (mine_ref, theirs_ref) = refs[:n], refs[n : 2 * n], refs[2 * n :]
     wanted, dim = sel_ref.shape
     half = wanted // 2
     rows = near_ref.shape[1] // 2
     got = got_ref[...].astype(jnp.float32)
-    chosen32 = sel_ref[...].astype(jnp.float32) + jnp.concatenate([got[half:], got[:half]], axis=0)
-    chosen = chosen32.astype(jnp.bfloat16)
-    cand_norm = column_sums(chosen32)[:1]
+    chosen = sel_ref[...].astype(jnp.float32) + jnp.concatenate([got[half:], got[:half]], axis=0)
+    cand_norm = column_sums(chosen)[:1]
+    twice = (chosen * -2.0).astype(jnp.bfloat16)
     sums = jnp.zeros((wanted, dim), jnp.float32)
     mass = jnp.zeros((8, wanted), jnp.float32)
-    for ref in block_refs:
-        block = ref[...]
-        wide = block.astype(jnp.float32)
-        norm = jnp.sum(wide * wide, axis=1, keepdims=True)
-        dots = lax.dot_general(block, chosen, LAST, preferred_element_type=jnp.float32)
-        dist = (norm + cand_norm) - 2.0 * dots
-        kern = jnp.exp(dist * -4.0).astype(jnp.bfloat16)
+    for block_ref, norm_ref in zip(block_refs, norm_refs):
+        block = block_ref[...]
+        norm = norm_ref[...]
+        dots = lax.dot_general(block, twice, LAST, preferred_element_type=jnp.float32)
+        dist = jnp.concatenate(
+            [
+                (norm[:, : min(LANES, wanted - w)] + cand_norm[:, w : w + LANES]) + dots[:, w : w + LANES]
+                for w in range(0, wanted, LANES)
+            ],
+            axis=1,
+        )
+        kern = jnp.exp2(dist * (-4.0 * math.log2(math.e))).astype(jnp.bfloat16)
         mass += jnp.sum(kern.astype(jnp.float32).reshape(rows // 8, 8, wanted), axis=0)
         sums += lax.dot_general(
             kern, block, (((0,), (0,)), ((), ())), preferred_element_type=jnp.float32
@@ -158,34 +205,33 @@
 
 
 SENDS = {
-    "sib": (None, "other"),
-    "z2": ("own", "two"),
+    "sib": ("own", "other"),
     "z1": ("own", "one"),
     "a0": ("own", "near"),
+    "z2": ("own", "two"),
     "b0": ("own", "far"),
     "e0": ("a0", "far"),
     "a1": ("z1", "near"),
     "b1": ("z1", "far"),
-    "e1": ("a1", "far"),
+    "e1": ("e0", "one"),
     "z3": ("z2", "one"),
     "a2": ("z2", "near"),
     "b2": ("z2", "far"),
-    "e2": ("a2", "far"),
+    "e2": ("z2", "diag"),
     "a3": ("z3", "near"),
     "b3": ("z3", "far"),
-    "e3": ("a3", "far"),
+    "e3": ("e2", "one"),
+    "got": ("sel", "other"),
 }
-ORDER = ("sib", "z2", "z1", "a0", "b0", "s0", "e0", "a1", "b1", "z3", "a2", "b2", "s1", "e1", "s2", "a3", "b3", "s3", "e2", "s4", "e3", "s5", "s6")
+ORDER = ("z1", "a0", "z2", "b0", "sib", "e0", "a1", "b1", "z3", "e2", "a2", "b2", "e1", "s1", "e3", "a3", "b3", "s3", "s5", "p6", "got", "n6")
 SCANS = {
-    "s0": ("own",),
-    "s1": ("a0", "b0", "z1"),
-    "s2": ("e0", "z2"),
-    "s3": ("a1", "b1", "e1", "z3"),
-    "s4": ("a2", "b2"),
-    "s5": ("a3", "b3", "e2"),
-    "s6": ("e3",),
+    "s1": ("own", "a0", "b0", "z1", "e0"),
+    "s3": ("z2", "a1", "b1", "e1", "z3"),
+    "s5": ("a2", "b2", "e2", "e3"),
+    "p6": ("a3", "b3"),
+    "n6": ("a3", "b3"),
 }
-BLOCKS = sum(SCANS.values(), ())
+BLOCKS = sum((names for scan, names in SCANS.items() if scan[0] != "p"), ())
 
 
 def gathered(chips, points, candidates, owner_slot):
@@ -202,84 +248,103 @@
         "two": lambda d, c: (d ^ 8) * 2 + c,
         "near": lambda d, c: (d ^ (1 if c == 0 else 2)) * 2 + c,
         "far": lambda d, c: (d ^ (2 if c == 0 else 1)) * 2 + c,
+        "diag": lambda d, c: (d ^ 3) * 2 + c,
     }
-    steps = {"one": 4, "two": 8, "near": near_bit, "far": far_bit}
-
-    flat = candidates.reshape(-1)
-    order = jnp.arange(2 * half, dtype=jnp.int32)
-    slot = jnp.where(order < half, (2 * d + c) * half + order, (2 * d + 1 - c) * half + order - half)
-    cand = jnp.sum(
-        jnp.where(owner_slot[None, :] == slot[:, None], flat[None, :], 0), axis=1, keepdims=True
-    )
-    span = 2 * chips * rows // LANES
-    low = (flat[None, :] % LANES == jnp.arange(LANES, dtype=jnp.int32)[:, None]).astype(jnp.bfloat16)
-    high = (flat[None, :] // LANES == jnp.arange(span, dtype=jnp.int32)[:, None]).astype(jnp.bfloat16)
-    hits = lax.dot_general(low, high, LAST, preferred_element_type=jnp.float32)
-    bias = jnp.where(hits > 0, 0.0, FAR).astype(jnp.float32)
-    origin = {"own": d}
+    steps = {"one": 4, "two": 8, "near": near_bit, "far": far_bit, "diag": 3, "other": 0}
+    origin = {"own": d, "sel": d}
     for name, (source, way) in SENDS.items():
-        if source:
-            origin[name] = origin[source] ^ steps[way]
+        origin[name] = origin[source] ^ steps[way]
     base = (jnp.stack([origin[name] for name in BLOCKS]) * 2 + c).astype(jnp.int32) * rows
+    meta = (jnp.stack([2 * d + c, 2 * d + 1 - c]) * half).astype(jnp.int32)
 
     smem = pl.BlockSpec(memory_space=pltpu.SMEM)
     vmem = pl.BlockSpec(memory_space=pltpu.VMEM)
     grant = pltpu.CompilerParams(vmem_limit_bytes=GRANT)
+    f32 = jnp.float32
     sel_shape = jax.ShapeDtypeStruct((2 * half, dim), jnp.bfloat16)
-    near_shape = jax.ShapeDtypeStruct((8, 2 * rows), jnp.float32)
-    norm_shape = jax.ShapeDtypeStruct((8, rows), jnp.float32)
-    blocks = {"own": points}
-    sel = near = norm = None
+    near_shape = jax.ShapeDtypeStruct((8, 2 * rows), f32)
+    total_shape = jax.ShapeDtypeStruct((8, rows), f32)
+    norm_shape = jax.ShapeDtypeStruct((rows, LANES), f32)
+
+    cand, bias = pl.pallas_call(
+        index_kernel,
+        out_shape=(
+            jax.ShapeDtypeStruct((2 * half, 1), jnp.int32),
+            jax.ShapeDtypeStruct((LANES, LANES), f32),
+        ),
+        in_specs=[smem, vmem, vmem],
+        out_specs=(vmem, vmem),
+        compiler_params=grant,
+        name="index_rows",
+    )(meta, candidates, owner_slot.reshape(1, total))
+
+    held = {"own": points}
+    norms = {}
+    near = own_norm = None
     for name in ORDER:
         if name in SENDS:
             source, way = SENDS[name]
-            blocks[name] = send(blocks[source or "own"], chips, targets[way])
+            held[name] = send(held[source], chips, targets[way])
             continue
         names = SCANS[name]
+        picks, scans = name[0] != "n", name[0] != "p"
+        first = "sel" not in held
+        operands = [base] + ([cand] if picks else []) + ([bias, points, held["sib"]] if scans else [])
+        operands += [held[b] for b in names]
+        if not first:
+            operands += ([held["sel"]] if picks else []) + ([near] if scans else [])
+        shapes = ([sel_shape] if picks else []) + ([near_shape] if scans else [])
+        shapes += ([total_shape] if first else []) + ([norm_shape] * len(names) if scans else [])
+        body = {"s": both_kernel, "p": pick_kernel, "n": near_kernel}[name[0]]
         work = len(names) * rows
-        first = sel is None
-        shapes = (sel_shape, near_shape) + ((norm_shape,) if first else ())
-        carried = () if first else (sel, near)
-        sel, near, *rest = pl.pallas_call(
-            functools.partial(scan_kernel, [BLOCKS.index(b) for b in names], first),
+        out = pl.pallas_call(
+            functools.partial(body, [BLOCKS.index(b) for b in names], first),
             out_shape=shapes,
-            in_specs=[smem] + [vmem] * (4 + len(names) + len(carried)),
-            out_specs=(vmem,) * len(shapes),
+            in_specs=[smem] + [vmem] * (len(operands) - 1),
+            out_specs=[vmem] * len(shapes),
             cost_estimate=pl.CostEstimate(
-                flops=4 * work * dim * (rows + half), bytes_accessed=work * dim, transcendentals=0
+                flops=4 * work * dim * (rows * scans + half * picks),
+                bytes_accessed=work * dim,
+                transcendentals=0,
             ),
             compiler_params=grant,
             name="scan_rows",
-        )(base, cand, bias, points, blocks["sib"], *[blocks[b] for b in names], *carried)
-        norm = rest[0] if first else norm
-
-    got = send(sel, chips, targets["other"])
+        )(*operands)
+        out = list(out)
+        if picks:
+            held["sel"] = out.pop(0)
+        if scans:
+            near = out.pop(0)
+            if first:
+                own_norm = out.pop(0)
+            norms.update(zip(names, out))
+
     deep = -(-(half + -(-rows // (dim + LANES))) // 8) * 8
     work = len(BLOCKS) * rows
     mine, theirs = pl.pallas_call(
         sum_kernel,
-        out_shape=(jax.ShapeDtypeStruct((deep, dim + LANES), jnp.float32),) * 2,
-        in_specs=[vmem] * (3 + len(BLOCKS)),
+        out_shape=(jax.ShapeDtypeStruct((deep, dim + LANES), f32),) * 2,
+        in_specs=[vmem] * (3 + 2 * len(BLOCKS)),
         out_specs=(vmem, vmem),
         cost_estimate=pl.CostEstimate(
             flops=8 * work * dim * half, bytes_accessed=work * dim * 2, transcendentals=work * 2 * half
         ),
         compiler_params=grant,
         name="sum_rows",
-    )(sel, got, near, *[blocks[b] for b in BLOCKS])
+    )(held["sel"], held["got"], near, *[held[b] for b in BLOCKS], *[norms[b] for b in BLOCKS])
     back = send(theirs, chips, targets["other"])
     centroids, masses, nearest = pl.pallas_call(
         finish_kernel,
         out_shape=(
-            jax.ShapeDtypeStruct((half, dim), jnp.float32),
-            jax.ShapeDtypeStruct((1, half), jnp.float32),
-            jax.ShapeDtypeStruct((1, rows), jnp.float32),
+            jax.ShapeDtypeStruct((half, dim), f32),
+            jax.ShapeDtypeStruct((1, half), f32),
+            jax.ShapeDtypeStruct((1, rows), f32),
         ),
         in_specs=[vmem] * 3,
         out_specs=(vmem,) * 3,
         compiler_params=grant,
         name="finish_rows",
-    )(mine, back, norm)
+    )(mine, back, own_norm)
     return centroids, masses.reshape(half), nearest.reshape(rows)
 
 

time: 58.3 us -> 52.9 us (0.907)
  waiting for transfers between devices: 19 us -> 9.25 us
  starting transfers between devices: 19.2 us -> 25.7 us
  matrix products: 1.19 us -> 0 us
  Pallas kernels: 15.8 us -> 14.9 us
    ppermute x18, waiting for transfers between devices: 19 us -> 9.25 us  [send(): return lax.ppermute(x, AXES, pairs)]
    ppermute x18, starting transfers between devices: 19.2 us -> 25.7 us  [send(): return lax.ppermute(x, AXES, pairs)]
    dot_general x1 -> x0, matrix products: 1.19 us -> none  [gathered(): hits = lax.dot_general(low, high, LAST, preferred_element_type=jnp.float32)]
    pallas_call x1, Pallas kernels: 4.05 us -> 3.11 us  [gathered(): pl.pallas_call(sum_kernel, out_shape=(jax.ShapeDtypeStruct((deep, dim + L...]
    broadcast_in_dim x2 -> x0, local copies, waits for them, and re-layouts: 0.84 us -> none  [the longest x1 0.72 us: gathered(): jnp.where(owner_slot[None, :] == slot[:, None], flat[None, :], 0)]
    unnamed x8, local copies, waits for them, and re-layouts: 0.85 us -> 1.68 us
    pallas_call x7 -> x6, Pallas kernels: 11 us -> 11.2 us  [the longest x5 9.88 us: gathered(): pl.pallas_call(functools.partial(body, [BLOCKS.index(b) for b in names],...]
  transfers between devices with their start and end apart: 18 -> 18, of which waited for: 8 -> 6; matrix products, arithmetic and copies ran while one was open for 4% -> 0% of each run, Pallas kernels for 17% -> 20%
where the time goes in v2:
time: 52.9 us; the launch traced here: 52.5 us
  starting transfers between devices  25.7 us (49%)
  Pallas kernels  14.9 us (28%)
  waiting for transfers between devices  9.25 us (17%)
  local copies, waits for them, and re-layouts  1.78 us (3%)
  between operations  0.79 us (1%)
    ppermute x18, starting transfers between devices, send(): return lax.ppermute(x, AXES, pairs)  25.7 us
    pallas_call x5, Pallas kernels, gathered(): pl.pallas_call(functools.partial(body, [BLOCKS.index(b) for b in names],...  9.88 us
    ppermute x18, waiting for transfers between devices, send(): return lax.ppermute(x, AXES, pairs)  9.25 us
    pallas_call x1, Pallas kernels, gathered(): pl.pallas_call(sum_kernel, out_shape=(jax.ShapeDtypeStruct((deep, dim + L...  3.11 us
    unnamed x8, local copies, waits for them, and re-layouts  1.68 us
    pallas_call x1, Pallas kernels, gathered(): pl.pallas_call(index_kernel, out_shape=(jax.ShapeDtypeStruct((2 * half, 1...  1.28 us
  transfers between devices with their start and end apart: 18, of which 6 were waited for; matrix products, arithmetic and copies ran while one was open for 0% of the time, Pallas kernels for 20%

profile of v2, /device:TPU:0, one launch (start us, length us, event | category | flops | bytes accessed | tf_op | source)
XLA Modules:
  0.0 52.5 jit_solution(16172724865502028792)
XLA Ops:
  0.6 3.0 %collective-permute-start.12 = (bf16[512,256]{1,0:T(8,128)(2,1)}, bf16[512,256]{1,0:T(8,128)(2,1)S(1)}, u32[]{:S(2)}, u32[]{:S(2)}) collective-permute-start(bf16[512,256]{1,0:T(8,128)(2,1)} %refs_0_.3), channel_id=1, source_target_pairs={{0,2},{1,5},{2,0},{3,7},{4,6},{5,1},{6,4},{7,3},{8,10},{9,13},{10,... | collective-permute-start | bytes 786440 | tf_op jit(solution)/shard_map/ppermute | solution.py:53
  3.7 1.6 %collective-permute-start.9 = (bf16[512,256]{1,0:T(8,128)(2,1)}, bf16[512,256]{1,0:T(8,128)(2,1)S(1)}, u32[]{:S(2)}, u32[]{:S(2)}) collective-permute-start(bf16[512,256]{1,0:T(8,128)(2,1)} %refs_0_.3), channel_id=1, source_target_pairs={{0,8},{1,9},{2,10},{3,11},{4,12},{5,13},{6,14},{7,15},{8,0},{9,1},... | collective-permute-start | bytes 786440 | tf_op jit(solution)/shard_map/ppermute | solution.py:53
  5.2 1.5 %collective-permute-start.15 = (bf16[512,256]{1,0:T(8,128)(2,1)}, bf16[512,256]{1,0:T(8,128)(2,1)S(1)}, u32[]{:S(2)}, u32[]{:S(2)}) collective-permute-start(bf16[512,256]{1,0:T(8,128)(2,1)} %refs_0_.3), channel_id=1, source_target_pairs={{0,4},{1,3},{2,6},{3,1},{4,0},{5,7},{6,2},{7,5},{8,12},{9,11},{10,... | collective-permute-start | bytes 786440 | tf_op jit(solution)/shard_map/ppermute | solution.py:53
  6.8 2.6 %collective-permute-start = (bf16[512,256]{1,0:T(8,128)(2,1)}, bf16[512,256]{1,0:T(8,128)(2,1)S(1)}, u32[]{:S(2)}, u32[]{:S(2)}) collective-permute-start(bf16[512,256]{1,0:T(8,128)(2,1)} %refs_0_.3), channel_id=1, source_target_pairs={{0,16},{1,17},{2,18},{3,19},{4,20},{5,21},{6,22},{7,23},{8,24},{9,... | collective-permute-start | bytes 786440 | tf_op jit(solution)/shard_map/ppermute | solution.py:53
  9.4 3.3 %collective-permute-start.13 = (bf16[512,256]{1,0:T(8,128)(2,1)S(1)}, bf16[512,256]{1,0:T(8,128)(2,1)S(1)}, u32[]{:S(2)}, u32[]{:S(2)}) collective-permute-start(bf16[512,256]{1,0:T(8,128)(2,1)S(1)} %collective-permute-done.12.refs_1_), channel_id=1, source_target_pairs={{0,4},{1,3},{2,6},{3,1},{4,0},{5,7},{6,2},{7,5},{8,12},{9,11},{10,... | collective-permute-start | bytes 786440 | tf_op jit(solution)/shard_map/ppermute | solution.py:53
  12.7 3.2 %collective-permute-done.9.refs_3_ = bf16[512,256]{1,0:T(8,128)(2,1)S(1)} collective-permute-done((bf16[512,256]{1,0:T(8,128)(2,1)}, bf16[512,256]{1,0:T(8,128)(2,1)S(1)}, u32[]{:S(2)}, u32[]{:S(2)}) %collective-permute-start.9) | collective-permute-done | bytes 262176 | tf_op jit(solution)/shard_map/ppermute | solution.py:53
  15.9 3.0 %collective-permute-start.10 = (bf16[512,256]{1,0:T(8,128)(2,1)S(1)}, bf16[512,256]{1,0:T(8,128)(2,1)S(1)}, u32[]{:S(2)}, u32[]{:S(2)}) collective-permute-start(bf16[512,256]{1,0:T(8,128)(2,1)S(1)} %collective-permute-done.9.refs_3_), channel_id=1, source_target_pairs={{0,2},{1,5},{2,0},{3,7},{4,6},{5,1},{6,4},{7,3},{8,10},{9,13},{10,... | collective-permute-start | bytes 786440 | tf_op jit(solution)/shard_map/ppermute | solution.py:53
  18.9 1.9 %collective-permute-done.refs_0_.refs_5_ = bf16[512,256]{1,0:T(8,128)(2,1)S(1)} collective-permute-done((bf16[512,256]{1,0:T(8,128)(2,1)}, bf16[512,256]{1,0:T(8,128)(2,1)S(1)}, u32[]{:S(2)}, u32[]{:S(2)}) %collective-permute-start) | collective-permute-done | bytes 262176 | tf_op jit(solution)/shard_map/ppermute | solution.py:53
  20.8 0.5 collective-permute-start.7
  21.2 0.1 add_multiply_fusion.meta_ref
  21.3 0.7 %copy-done.2 = s32[4,768]{1,0:T(4,128)S(1)} copy-done((s32[4,768]{1,0:T(4,128)S(1)}, s32[4,768]{1,0:T(4,128)}, u32[]{:S(2)}) %copy-start.2) | copy-done | bytes 12312
  22.0 1.3 %index_rows.1 = (s32[192,1]{1,0:T(8,128)S(1)}, f32[128,128]{1,0:T(8,128)S(1)}) custom-call(s32[2]{0:T(128)S(1)} %add_multiply_fusion.meta_ref, s32[4,768]{1,0:T(4,128)S(1)} %copy-done.2, s32[1,3072]{1,0:T(1,128)S(1)} %bitcast.21), custom_call_target="tpu_custom_call" | custom-call | tf_op jit(solution)/shard_map/index_rows/pallas_call | solution.py:269
  23.3 0.1 stack.76
  23.4 0.2 collective-permute-start.1
  23.7 1.9 %collective-permute-start.14 = (bf16[512,256]{1,0:T(8,128)(2,1)S(1)}, bf16[512,256]{1,0:T(8,128)(2,1)S(1)}, u32[]{:S(2)}, u32[]{:S(2)}) collective-permute-start(bf16[512,256]{1,0:T(8,128)(2,1)S(1)} %collective-permute-done.13.refs_4_), channel_id=1, source_target_pairs={{0,8},{1,9},{2,10},{3,11},{4,12},{5,13},{6,14},{7,15},{8,0},{9,1},... | collective-permute-start | bytes 786440 | tf_op jit(solution)/shard_map/ppermute | solution.py:53
  25.5 0.3 collective-permute-done.11.refs_2_.refs_7_
  25.9 1.2 %collective-permute-start.6 = (bf16[512,256]{1,0:T(8,128)(2,1)S(1)}, bf16[512,256]{1,0:T(8,128)(2,1)S(1)}, u32[]{:S(2)}, u32[]{:S(2)}) collective-permute-start(bf16[512,256]{1,0:T(8,128)(2,1)S(1)} %collective-permute-done.refs_0_.refs_5_), channel_id=1, source_target_pairs={{0,4},{1,3},{2,6},{3,1},{4,0},{5,7},{6,2},{7,5},{8,12},{9,11},{10,... | collective-permute-start | bytes 786440 | tf_op jit(solution)/shard_map/ppermute | solution.py:53
  27.1 3.1 %collective-permute-start.5 = (bf16[512,256]{1,0:T(8,128)(2,1)S(1)}, bf16[512,256]{1,0:T(8,128)(2,1)S(1)}, u32[]{:S(2)}, u32[]{:S(2)}) collective-permute-start(bf16[512,256]{1,0:T(8,128)(2,1)S(1)} %collective-permute-done.refs_0_.refs_5_), channel_id=1, source_target_pairs={{0,2},{1,5},{2,0},{3,7},{4,6},{5,1},{6,4},{7,3},{8,10},{9,13},{10,... | collective-permute-start | bytes 786440 | tf_op jit(solution)/shard_map/ppermute | solution.py:53
  30.2 2.1 %collective-permute-done.7.refs_2_.refs_12_ = bf16[512,256]{1,0:T(8,128)(2,1)S(1)} collective-permute-done((bf16[512,256]{1,0:T(8,128)(2,1)S(1)}, bf16[512,256]{1,0:T(8,128)(2,1)S(1)}, u32[]{:S(2)}, u32[]{:S(2)}) %collective-permute-start.7) | collective-permute-done | bytes 262176 | tf_op jit(solution)/shard_map/ppermute | solution.py:53
  32.3 0.9 %copy-done = bf16[512,256]{1,0:T(8,128)(2,1)S(1)} copy-done((bf16[512,256]{1,0:T(8,128)(2,1)S(1)}, bf16[512,256]{1,0:T(8,128)(2,1)}, u32[]{:S(2)}) %copy-start) | copy-done | bytes 262168
  33.2 2.7 %scan_rows.5 = (bf16[192,256]{1,0:T(8,128)(2,1)S(1)}, f32[8,1024]{1,0:T(8,128)S(1)}, f32[8,512]{1,0:T(8,128)S(1)}, f32[512,128]{1,0:T(8,128)S(1)}, f32[512,128]{...) custom-call(s32[16]{0:T(128)S(1)} %add_multiply_fusion.1.base_ref, ...), custom_call_target="tpu_custom_call" | custom-call | flops 1593835520 | bytes 655360 | tf_op jit(solution)/shard_map/scan_rows/pallas_call | solution.py:300
  35.9 1.7 %collective-permute-start.3 = (bf16[512,256]{1,0:T(8,128)(2,1)S(1)}, bf16[512,256]{1,0:T(8,128)(2,1)S(1)}, u32[]{:S(2)}, u32[]{:S(2)}) collective-permute-start(bf16[512,256]{1,0:T(8,128)(2,1)S(1)} %collective-permute-done.1.refs_4_.refs_9_), channel_id=1, source_target_pairs={{0,4},{1,3},{2,6},{3,1},{4,0},{5,7},{6,2},{7,5},{8,12},{9,11},{10,... | collective-permute-start | bytes 786440 | tf_op jit(solution)/shard_map/ppermute | solution.py:53
  37.6 0.7 %collective-permute-done.14.refs_3_.refs_8_ = bf16[512,256]{1,0:T(8,128)(2,1)S(1)} collective-permute-done((bf16[512,256]{1,0:T(8,128)(2,1)S(1)}, bf16[512,256]{1,0:T(8,128)(2,1)S(1)}, u32[]{:S(2)}, u32[]{:S(2)}) %collective-permute-start.14) | collective-permute-done | bytes 262176 | tf_op jit(solution)/shard_map/ppermute | solution.py:53
  38.3 1.5 %collective-permute-start.2 = (bf16[512,256]{1,0:T(8,128)(2,1)S(1)}, bf16[512,256]{1,0:T(8,128)(2,1)S(1)}, u32[]{:S(2)}, u32[]{:S(2)}) collective-permute-start(bf16[512,256]{1,0:T(8,128)(2,1)S(1)} %collective-permute-done.1.refs_4_.refs_9_), channel_id=1, source_target_pairs={{0,2},{1,5},{2,0},{3,7},{4,6},{5,1},{6,4},{7,3},{8,10},{9,13},{10,... | collective-permute-start | bytes 786440 | tf_op jit(solution)/shard_map/ppermute | solution.py:53
  39.8 2.6 %scan_rows.6 = (bf16[192,256]{1,0:T(8,128)(2,1)S(1)}, f32[8,1024]{1,0:T(8,128)S(1)}, f32[512,128]{1,0:T(8,128)S(1)}, f32[512,128]{1,0:T(8,128)S(1)}, f32[512,128...) custom-call(s32[16]{0:T(128)S(1)} %add_multiply_fusion.1.base_ref, ...), custom_call_target="tpu_custom_call" | custom-call | flops 1593835520 | bytes 655360 | tf_op jit(solution)/shard_map/scan_rows/pallas_call | solution.py:300
  42.5 2.2 %scan_rows.7 = (bf16[192,256]{1,0:T(8,128)(2,1)S(1)}, f32[8,1024]{1,0:T(8,128)S(1)}, f32[512,128]{1,0:T(8,128)S(1)}, f32[512,128]{1,0:T(8,128)S(1)}, f32[512,128]{1,0:T(8,128)S(1)}, /*index=5*/f32[512,128]{1,0:T(8,128)S(1)}) custom-call(s32[16]{0:T(128)S(1)} %add_multiply_fusion.1.base_ref, s32[192,1]{1,0:T(8,128)S(1)} %get-tuple-element.34.cand_ref, ...), custom_call_target="tpu_custom_call" | custom-call | flops 1275068416 | bytes 524288 | tf_op jit(solution)/shard_map/scan_rows/pallas_call | solution.py:300
  44.7 0.9 %scan_rows.8.sel_ref = bf16[192,256]{1,0:T(8,128)(2,1)S(1)} custom-call(s32[16]{0:T(128)S(1)} %add_multiply_fusion.1.base_ref, s32[192,1]{1,0:T(8,128)S(1)} %get-tuple-element.34.cand_ref, bf16[512,256]{1,0:T(8,128)(2,1)S(1)} %collective-permute-done.2.refs_0_.refs_14_, bf16[512,256]{1,0:T(8,128)(2,1)S(1)} %collective-permute-done.3.refs_1_.refs_15_, ...), custom_call_target="tpu_custom_call" | custom-call | flops 100663296 | bytes 262144 | tf_op jit(solution)/shard_map/scan_rows/pallas_call | solution.py:300
  45.7 1.5 %scan_rows.9 = (f32[8,1024]{1,0:T(8,128)S(1)}, f32[512,128]{1,0:T(8,128)S(1)}, f32[512,128]{1,0:T(8,128)S(1)}) custom-call(s32[16]{0:T(128)S(1)} %add_multiply_fusion.1.base_ref, f32[128,128]{1,0:T(8,128)S(1)} %get-tuple-element.35.bias_ref, bf16[512,256]{1,0:T(8,128)(2,1)S(1)} %copy-done.1, bf16[512,256]{1,0:T(8,128)(2,1)S(1)} %collective-permute-done.4.sib_ref, ...), custom_call_target="tpu_custom_call" | custom-call | flops 536870912 | bytes 262144 | tf_op jit(solution)/shard_map/scan_rows/pallas_call | solution.py:300
  47.2 3.1 %sum_rows.1 = (f32[104,384]{1,0:T(8,128)S(1)}, f32[104,384]{1,0:T(8,128)S(1)}) custom-call(bf16[192,256]{1,0:T(8,128)(2,1)S(1)} %scan_rows.8.sel_ref, bf16[192,256]{1,0:T(8,128)(2,1)S(1)} %collective-permute-done.16.got_ref, f32[8,1024]{1,0:T(8,128)S(1)} %get-tuple-element.42.near_ref, bf16[512,256]{1,0:T(8,128)(2,1)S(1)} %copy-done.1, ...), custom_call_target="tpu_custom_call" | custom-call | flops 1610612736 | bytes 4194304 | tf_op jit(solution)/shard_map/sum_rows/pallas_call | solution.py:324
  50.3 0.6 %collective-permute-start.17 = (f32[104,384]{1,0:T(8,128)S(1)}, f32[104,384]{1,0:T(8,128)S(1)}, u32[]{:S(2)}, u32[]{:S(2)}) collective-permute-start(f32[104,384]{1,0:T(8,128)S(1)} %get-tuple-element.60), channel_id=1, source_target_pairs={{0,1},{1,0},{2,3},{3,2},{4,5},{5,4},{6,7},{7,6},{8,9},{9,8},{10,11... | collective-permute-start | bytes 479240 | tf_op jit(solution)/shard_map/ppermute | solution.py:53
  50.9 1.0 %collective-permute-done.17.back_ref = f32[104,384]{1,0:T(8,128)S(1)} collective-permute-done((f32[104,384]{1,0:T(8,128)S(1)}, f32[104,384]{1,0:T(8,128)S(1)}, u32[]{:S(2)}, u32[]{:S(2)}) %collective-permute-start.17) | collective-permute-done | bytes 159776 | tf_op jit(solution)/shard_map/ppermute | solution.py:53
  51.9 0.7 %finish_rows.1 = (f32[96,256]{1,0:T(8,128)}, f32[1,96]{1,0:T(1,128)}, f32[1,512]{1,0:T(1,128)}) custom-call(f32[104,384]{1,0:T(8,128)S(1)} %get-tuple-element.59.mine_ref, f32[104,384]{1,0:T(8,128)S(1)} %collective-permute-done.17.back_ref, f32[8,512]{1,0:T(8,128)S(1)} %get-tuple-element.61.norm_ref), custom_call_target="tpu_custom_call" | custom-call | tf_op jit(solution)/shard_map/finish_rows/pallas_call | solution.py:336
  (23 shorter events, 0.1 us)
Async XLA Ops:
  0.6 8.7 %collective-permute-start.12 = (bf16[512,256]{1,0:T(8,128)(2,1)}, bf16[512,256]{1,0:T(8,128)(2,1)S(1)}, u32[]{:S(2)}, u32[]{:S(2)}) collective-permute-start(bf16[512,256]{1,0:T(8,128)(2,1)} %refs_0_.3), channel_id=1, source_target_pairs={{0,2},{1,5},{2,0},{3,7},{4,6},{5,1},{6,4},{7,3},{8,10},{9,13},{10,... | collective-permute-start | bytes 786440 | tf_op jit(solution)/shard_map/ppermute | solution.py:53
  3.7 12.3 %collective-permute-start.9 = (bf16[512,256]{1,0:T(8,128)(2,1)}, bf16[512,256]{1,0:T(8,128)(2,1)S(1)}, u32[]{:S(2)}, u32[]{:S(2)}) collective-permute-start(bf16[512,256]{1,0:T(8,128)(2,1)} %refs_0_.3), channel_id=1, source_target_pairs={{0,8},{1,9},{2,10},{3,11},{4,12},{5,13},{6,14},{7,15},{8,0},{9,1},... | collective-permute-start | bytes 786440 | tf_op jit(solution)/shard_map/ppermute | solution.py:53
  5.2 10.7 %collective-permute-start.15 = (bf16[512,256]{1,0:T(8,128)(2,1)}, bf16[512,256]{1,0:T(8,128)(2,1)S(1)}, u32[]{:S(2)}, u32[]{:S(2)}) collective-permute-start(bf16[512,256]{1,0:T(8,128)(2,1)} %refs_0_.3), channel_id=1, source_target_pairs={{0,4},{1,3},{2,6},{3,1},{4,0},{5,7},{6,2},{7,5},{8,12},{9,11},{10,... | collective-permute-start | bytes 786440 | tf_op jit(solution)/shard_map/ppermute | solution.py:53
  6.8 14.0 %collective-permute-start = (bf16[512,256]{1,0:T(8,128)(2,1)}, bf16[512,256]{1,0:T(8,128)(2,1)S(1)}, u32[]{:S(2)}, u32[]{:S(2)}) collective-permute-start(bf16[512,256]{1,0:T(8,128)(2,1)} %refs_0_.3), channel_id=1, source_target_pairs={{0,16},{1,17},{2,18},{3,19},{4,20},{5,21},{6,22},{7,23},{8,24},{9,... | collective-permute-start | bytes 786440 | tf_op jit(solution)/shard_map/ppermute | solution.py:53
  9.3 14.1 %collective-permute-start.4 = (bf16[512,256]{1,0:T(8,128)(2,1)}, bf16[512,256]{1,0:T(8,128)(2,1)S(1)}, u32[]{:S(2)}, u32[]{:S(2)}) collective-permute-start(bf16[512,256]{1,0:T(8,128)(2,1)} %refs_0_.3), channel_id=1, source_target_pairs={{0,1},{1,0},{2,3},{3,2},{4,5},{5,4},{6,7},{7,6},{8,9},{9,8},{10,11... | collective-permute-start | bytes 786440 | tf_op jit(solution)/shard_map/ppermute | solution.py:53
  9.4 14.3 %collective-permute-start.13 = (bf16[512,256]{1,0:T(8,128)(2,1)S(1)}, bf16[512,256]{1,0:T(8,128)(2,1)S(1)}, u32[]{:S(2)}, u32[]{:S(2)}) collective-permute-start(bf16[512,256]{1,0:T(8,128)(2,1)S(1)} %collective-permute-done.12.refs_1_), channel_id=1, source_target_pairs={{0,4},{1,3},{2,6},{3,1},{4,0},{5,7},{6,2},{7,5},{8,12},{9,11},{10,... | collective-permute-start | bytes 786440 | tf_op jit(solution)/shard_map/ppermute | solution.py:53
  15.9 9.9 %collective-permute-start.11 = (bf16[512,256]{1,0:T(8,128)(2,1)S(1)}, bf16[512,256]{1,0:T(8,128)(2,1)S(1)}, u32[]{:S(2)}, u32[]{:S(2)}) collective-permute-start(bf16[512,256]{1,0:T(8,128)(2,1)S(1)} %collective-permute-done.9.refs_3_), channel_id=1, source_target_pairs={{0,4},{1,3},{2,6},{3,1},{4,0},{5,7},{6,2},{7,5},{8,12},{9,11},{10,... | collective-permute-start | bytes 786440 | tf_op jit(solution)/shard_map/ppermute | solution.py:53
  15.9 11.1 %collective-permute-start.10 = (bf16[512,256]{1,0:T(8,128)(2,1)S(1)}, bf16[512,256]{1,0:T(8,128)(2,1)S(1)}, u32[]{:S(2)}, u32[]{:S(2)}) collective-permute-start(bf16[512,256]{1,0:T(8,128)(2,1)S(1)} %collective-permute-done.9.refs_3_), channel_id=1, source_target_pairs={{0,2},{1,5},{2,0},{3,7},{4,6},{5,1},{6,4},{7,3},{8,10},{9,13},{10,... | collective-permute-start | bytes 786440 | tf_op jit(solution)/shard_map/ppermute | solution.py:53
  20.8 11.5 %collective-permute-start.7 = (bf16[512,256]{1,0:T(8,128)(2,1)S(1)}, bf16[512,256]{1,0:T(8,128)(2,1)S(1)}, u32[]{:S(2)}, u32[]{:S(2)}) collective-permute-start(bf16[512,256]{1,0:T(8,128)(2,1)S(1)} %collective-permute-done.refs_0_.refs_5_), channel_id=1, source_target_pairs={{0,6},{1,7},{2,4},{3,5},{4,2},{5,3},{6,0},{7,1},{8,14},{9,15},{10,... | collective-permute-start | bytes 786440 | tf_op jit(solution)/shard_map/ppermute | solution.py:53
  21.3 0.7 %copy-start.2 = (s32[4,768]{1,0:T(4,128)S(1)}, s32[4,768]{1,0:T(4,128)}, u32[]{:S(2)}) copy-start(s32[4,768]{1,0:T(4,128)} %cand_ref.1) | copy-start | bytes 36868
  21.3 0.7 %copy-start.3 = (s32[3072]{0:T(1024)S(1)}, s32[3072]{0:T(1024)}, u32[]{:S(2)}) copy-start(s32[3072]{0:T(1024)} %param.5) | copy-start | bytes 36868
  23.4 12.4 %collective-permute-start.1 = (bf16[512,256]{1,0:T(8,128)(2,1)S(1)}, bf16[512,256]{1,0:T(8,128)(2,1)S(1)}, u32[]{:S(2)}, u32[]{:S(2)}) collective-permute-start(bf16[512,256]{1,0:T(8,128)(2,1)S(1)} %collective-permute-done.refs_0_.refs_5_), channel_id=1, source_target_pairs={{0,8},{1,9},{2,10},{3,11},{4,12},{5,13},{6,14},{7,15},{8,0},{9,1},... | collective-permute-start | bytes 786440 | tf_op jit(solution)/shard_map/ppermute | solution.py:53
  23.7 14.6 %collective-permute-start.14 = (bf16[512,256]{1,0:T(8,128)(2,1)S(1)}, bf16[512,256]{1,0:T(8,128)(2,1)S(1)}, u32[]{:S(2)}, u32[]{:S(2)}) collective-permute-start(bf16[512,256]{1,0:T(8,128)(2,1)S(1)} %collective-permute-done.13.refs_4_), channel_id=1, source_target_pairs={{0,8},{1,9},{2,10},{3,11},{4,12},{5,13},{6,14},{7,15},{8,0},{9,1},... | collective-permute-start | bytes 786440 | tf_op jit(solution)/shard_map/ppermute | solution.py:53
  25.9 16.6 %collective-permute-start.6 = (bf16[512,256]{1,0:T(8,128)(2,1)S(1)}, bf16[512,256]{1,0:T(8,128)(2,1)S(1)}, u32[]{:S(2)}, u32[]{:S(2)}) collective-permute-start(bf16[512,256]{1,0:T(8,128)(2,1)S(1)} %collective-permute-done.refs_0_.refs_5_), channel_id=1, source_target_pairs={{0,4},{1,3},{2,6},{3,1},{4,0},{5,7},{6,2},{7,5},{8,12},{9,11},{10,... | collective-permute-start | bytes 786440 | tf_op jit(solution)/shard_map/ppermute | solution.py:53
  27.1 15.4 %collective-permute-start.5 = (bf16[512,256]{1,0:T(8,128)(2,1)S(1)}, bf16[512,256]{1,0:T(8,128)(2,1)S(1)}, u32[]{:S(2)}, u32[]{:S(2)}) collective-permute-start(bf16[512,256]{1,0:T(8,128)(2,1)S(1)} %collective-permute-done.refs_0_.refs_5_), channel_id=1, source_target_pairs={{0,2},{1,5},{2,0},{3,7},{4,6},{5,1},{6,4},{7,3},{8,10},{9,13},{10,... | collective-permute-start | bytes 786440 | tf_op jit(solution)/shard_map/ppermute | solution.py:53
  32.2 10.2 %collective-permute-start.8 = (bf16[512,256]{1,0:T(8,128)(2,1)S(1)}, bf16[512,256]{1,0:T(8,128)(2,1)S(1)}, u32[]{:S(2)}, u32[]{:S(2)}) collective-permute-start(bf16[512,256]{1,0:T(8,128)(2,1)S(1)} %collective-permute-done.7.refs_2_.refs_12_), channel_id=1, source_target_pairs={{0,8},{1,9},{2,10},{3,11},{4,12},{5,13},{6,14},{7,15},{8,0},{9,1},... | collective-permute-start | bytes 786440 | tf_op jit(solution)/shard_map/ppermute | solution.py:53
  32.2 1.0 %copy-start = (bf16[512,256]{1,0:T(8,128)(2,1)S(1)}, bf16[512,256]{1,0:T(8,128)(2,1)}, u32[]{:S(2)}) copy-start(bf16[512,256]{1,0:T(8,128)(2,1)} %refs_0_.3) | copy-start | bytes 786436
  35.9 8.8 %collective-permute-start.3 = (bf16[512,256]{1,0:T(8,128)(2,1)S(1)}, bf16[512,256]{1,0:T(8,128)(2,1)S(1)}, u32[]{:S(2)}, u32[]{:S(2)}) collective-permute-start(bf16[512,256]{1,0:T(8,128)(2,1)S(1)} %collective-permute-done.1.refs_4_.refs_9_), channel_id=1, source_target_pairs={{0,4},{1,3},{2,6},{3,1},{4,0},{5,7},{6,2},{7,5},{8,12},{9,11},{10,... | collective-permute-start | bytes 786440 | tf_op jit(solution)/shard_map/ppermute | solution.py:53
  38.3 6.4 %collective-permute-start.2 = (bf16[512,256]{1,0:T(8,128)(2,1)S(1)}, bf16[512,256]{1,0:T(8,128)(2,1)S(1)}, u32[]{:S(2)}, u32[]{:S(2)}) collective-permute-start(bf16[512,256]{1,0:T(8,128)(2,1)S(1)} %collective-permute-done.1.refs_4_.refs_9_), channel_id=1, source_target_pairs={{0,2},{1,5},{2,0},{3,7},{4,6},{5,1},{6,4},{7,3},{8,10},{9,13},{10,... | collective-permute-start | bytes 786440 | tf_op jit(solution)/shard_map/ppermute | solution.py:53
  44.7 1.0 %copy-start.1 = (bf16[512,256]{1,0:T(8,128)(2,1)S(1)}, bf16[512,256]{1,0:T(8,128)(2,1)}, u32[]{:S(2)}) copy-start(bf16[512,256]{1,0:T(8,128)(2,1)} %refs_0_.3) | copy-start | bytes 786436
  45.6 1.6 %collective-permute-start.16 = (bf16[192,256]{1,0:T(8,128)(2,1)S(1)}, bf16[192,256]{1,0:T(8,128)(2,1)S(1)}, u32[]{:S(2)}, u32[]{:S(2)}) collective-permute-start(bf16[192,256]{1,0:T(8,128)(2,1)S(1)} %scan_rows.8.sel_ref), channel_id=1, source_target_pairs={{0,1},{1,0},{2,3},{3,2},{4,5},{5,4},{6,7},{7,6},{8,9},{9,8},{10,11... | collective-permute-start | bytes 294920 | tf_op jit(solution)/shard_map/ppermute | solution.py:53
  50.3 1.6 %collective-permute-start.17 = (f32[104,384]{1,0:T(8,128)S(1)}, f32[104,384]{1,0:T(8,128)S(1)}, u32[]{:S(2)}, u32[]{:S(2)}) collective-permute-start(f32[104,384]{1,0:T(8,128)S(1)} %get-tuple-element.60), channel_id=1, source_target_pairs={{0,1},{1,0},{2,3},{3,2},{4,5},{5,4},{6,7},{7,6},{8,9},{9,8},{10,11... | collective-permute-start | bytes 479240 | tf_op jit(solution)/shard_map/ppermute | solution.py:53
